TPU v7x, 32 devices: a whole 2x2x4 slice. The times are simulated.
32 devices in a mesh: slab: 8 (over z, y), grp: 4 (over x, core).
Axes of the slice: x: 2, y: 2, z: 4, core: 2. Of those that a mesh axis runs over, the one named last changes fastest.
Arguments:
- potential: bfloat16 [64, 8, 1024], P('slab'), may hold values from -3 to 3
- coefficients: bfloat16 [128, 16, 8, 1024], P(('slab', 'grp')), may hold values from -1 to 1
- box_center: int32 [128], replicated, may hold values from 0 to 63, as said below
- box_extent: int32 [128], replicated, may hold values from 8 to 16
Outputs:
- margin: float32 [128, 80], P(('slab', 'grp'))
- hamiltonian: float32 [128, 80], P(('slab', 'grp'))
Inputs may be any that keep to these rules, and one draw needn't show every extreme that they name: `box_center`: function b's centre lies among the 8 planes of slab b // 16, that is from (8 * (b // 16)) on.
All inputs are finite; a program needn't handle non-finite values.
Results may differ from a plain program's by a relative error of at most 0.0003.
Values may be sent and summed in bfloat16 or wider, within the bound.
A program may use at most 64 MiB of HBM per device.

v0:
```python
import functools

import jax
import jax.numpy as jnp
import numpy as np
from jax import lax
from jax.experimental import pallas as pl
from jax.experimental.pallas import tpu as pltpu
from jax.sharding import PartitionSpec as P

COMP = 8
CX = 32
CY = 32
MESH = pl.DeviceIdType.MESH


def haar_signs():
    ids = np.arange(COMP)
    common = ids[:, None] & ids[None, :]
    parity = (common % 2 + common // 2 % 2 + common // 4 % 2) % 2
    return (1 - 2 * parity).astype(np.float32)


def matrices(members, per, seg):
    rows = members * COMP
    order = np.zeros((COMP, members, members, COMP), np.float32)
    haar = np.zeros((COMP, members, members, COMP), np.float32)
    signs = haar_signs()
    half = per // 2
    pick = np.zeros((COMP, members, members // 2, COMP), np.float32)
    for n in range(members):
        group, func = divmod(n, per)
        for c in range(COMP):
            order[c, n, n, c] = 1.0
            haar[c, n, n, :] = signs[c]
            pick[c, n, group * half + func % half, c] = 1.0
    stacked = np.concatenate([order.reshape(rows, rows), haar.reshape(rows, rows)], 0)
    lap = np.zeros((seg + 128, seg), np.float32)
    for i in range(seg):
        lap[i, i] = 3.0
        if i % CY:
            lap[i - 1, i] = -0.5
            lap[i, i - 1] = -0.5
        if i >= CY:
            lap[i - CY, i] = -0.5
            lap[i, i - CY] = -0.5
    for i in range(CY):
        lap[seg + 128 - CY + i, i] = -0.5
        lap[seg + 64 - CY + i, i] = -0.5
        lap[seg + i, seg - CY + i] = -0.5
        lap[seg + 64 + i, seg - CY + i] = -0.5
    as_bf16 = lambda value: jnp.asarray(value, jnp.bfloat16)
    return as_bf16(stacked), as_bf16(pick.reshape(rows, -1)), as_bf16(lap)


def band_kernel(
    slabs,
    groups,
    depth,
    coef_ref,
    pot_ref,
    center_ref,
    extent_ref,
    order_ref,
    pick_ref,
    lap_ref,
    out_ref,
    main,
    halo,
    got,
    got_halo,
    got_pot,
    orb,
    app,
    limits,
    rows,
    got_rows,
    send_main,
    send_halo,
    send_pot,
    send_rows,
    recv_main,
    recv_halo,
    recv_pot,
    recv_rows,
):
    slab = lax.axis_index("slab")
    me = lax.axis_index("grp")
    per, box, comp, cells = coef_ref.shape
    seg = cells // groups
    half = per // 2
    members = groups * per
    odd = lax.rem(slab, 2)
    partner = slab + 1 - 2 * odd
    ahead = lax.rem(slab + 2, slabs)
    behind = lax.rem(slab + slabs - 2, slabs)
    is_odd = odd == 1
    slots = [2 * odd, 1, 2 - 2 * odd]
    frame_to = [slab, partner, lax.select(is_odd, ahead, behind)]
    rows_to = [slab, partner, lax.select(is_odd, behind, ahead)]
    relayed = (0, 1) if groups == 4 else ()
    direct = tuple(step for step in range(groups) if step not in relayed)
    if groups == 4:
        targets = [lax.rem(me + 2, groups), 3 - me, me + 1 - 2 * lax.rem(me, 2), me]
    else:
        targets = [lax.rem(me + 1 + step, groups) for step in range(groups)]

    barrier = pltpu.get_barrier_semaphore()
    for to in targets:
        for place in (slab, partner, ahead, behind):
            if place is slab and to is targets[-1]:
                continue
            pl.semaphore_signal(barrier, inc=1, device_id=(place, to), device_id_type=MESH)

    lane = lax.broadcasted_iota(jnp.int32, (comp, 128), 1)
    first = (slab * groups + me) * per
    extents = [extent_ref[first + f] for f in range(per)]
    starts = [
        center_ref[first + f] - slab * depth - lax.shift_right_logical(extents[f], 1)
        for f in range(per)
    ]

    def build(kind, j, with_halo):
        planes = []
        for f in range(per):
            p = j - 1 - starts[f]
            if kind == 0:
                p = p + depth
                p = jnp.where(p < extents[f], p, p - 2 * depth)
            inside = (p >= 0) & (p < extents[f])
            value = coef_ref[f, jnp.clip(p, 0, box - 1)].astype(jnp.float32)
            planes.append(jnp.where(inside, value, 0.0))
        for g in range(groups):
            at = slice(g * seg, (g + 1) * seg)
            main[kind, g, j] = jnp.concatenate([v[:, at] for v in planes], 0).astype(
                jnp.bfloat16
            )
            if not with_halo:
                continue
            tiles = []
            for v in planes:
                zero = jnp.zeros((comp, 128), jnp.float32)
                before = v[:, g * seg - 128 : g * seg] if g else zero
                after = v[:, (g + 1) * seg : (g + 1) * seg + 128] if g < groups - 1 else zero
                tiles.append(
                    jnp.where(lane >= 128 - CY, before, jnp.where(lane < CY, after, 0.0))
                )
            packed = [tiles[f] + pltpu.roll(tiles[half + f], 64, 1) for f in range(half)]
            halo[kind, g, j - 1] = jnp.concatenate(packed, 0).astype(jnp.bfloat16)

    def build_set(kind):
        @pl.loop(1, depth + 1)
        def _(j):
            build(kind, j, True)

        build(kind, 0, False)
        build(kind, depth + 1, False)

    unsent = []

    def move(role, step, source, target, send, recv, to):
        if role == 0 and step == groups - 1:
            pltpu.make_async_copy(source, target, recv).start()
            return
        copy = pltpu.make_async_remote_copy(
            src_ref=source,
            dst_ref=target,
            send_sem=send.at[role, step],
            recv_sem=recv,
            device_id=to,
            device_id_type=MESH,
        )
        copy.start()
        unsent.append(copy)

    def send(role, step):
        to, kind = targets[step], role % 2
        for source, target, sem, recv in (
            (main, got, send_main, recv_main),
            (halo, got_halo, send_halo, recv_halo),
        ):
            move(
                role,
                step,
                source.at[kind, to],
                target.at[role, me],
                sem,
                recv.at[role, me],
                (frame_to[role], to),
            )

    def arrived(role, g):
        for target, recv in ((got, recv_main), (got_halo, recv_halo)):
            block = target.at[role, g]
            pltpu.make_async_copy(block, block, recv.at[role, g]).wait()

    def relay(step):
        source = targets[step]
        for block, sem, recv in (
            (got, send_main, recv_main),
            (got_halo, send_halo, recv_halo),
        ):
            move(
                2,
                step,
                block.at[0, source],
                block.at[2, source],
                sem,
                recv.at[2, source],
                (frame_to[2], me),
            )

    pot_copy = pltpu.make_async_remote_copy(
        src_ref=pot_ref.at[:, :, pl.ds(pl.multiple_of(me * seg, seg), seg)],
        dst_ref=got_pot,
        send_sem=send_pot,
        recv_sem=recv_pot,
        device_id=(partner, me),
        device_id_type=MESH,
    )

    build_set(0)
    pl.semaphore_wait(barrier, 4 * groups - 1)
    build_set(1)
    for step in relayed:
        send(0, step)
    for step in direct:
        send(2, step)
    for step in direct:
        send(0, step)
    pot_copy.start()

    member = lax.broadcasted_iota(jnp.int32, (members, seg), 0)
    for slot in range(3):
        home = lax.rem(partner + slot - 1 + slabs, slabs)
        begin = jnp.zeros((members, seg), jnp.int32)
        end = jnp.zeros((members, seg), jnp.int32)
        for n in range(members):
            extent = extent_ref[home * members + n]
            start = (
                center_ref[home * members + n]
                - home * depth
                - lax.shift_right_logical(extent, 1)
                + (slot - 1) * depth
            )
            begin = jnp.where(member == n, start, begin)
            end = jnp.where(member == n, start + extent, end)
        limits[slot, 0] = begin
        limits[slot, 1] = end

    for step in (*direct, *relayed):
        send(1, step)
    for step in relayed:
        arrived(0, targets[step])
        relay(step)
    pot_copy.wait_recv()

    at_lane = lax.broadcasted_iota(jnp.int32, (members * COMP, 128), 1)
    func = lax.rem(lax.broadcasted_iota(jnp.int32, (members * COMP, 128), 0), per)
    keep = ((at_lane < CY) | (at_lane >= 128 - CY)) == (func < half)

    for role in range(3):
        slot = slots[role]
        for step in direct if role == 0 else range(groups):
            arrived(role, targets[step])

        @pl.loop(0, depth + 2, unroll=(depth + 2) // 2)
        def _(j):
            x = got[role, :, j].reshape(members * COMP, seg)
            turned = jnp.dot(
                order_ref[: members * COMP], x, preferred_element_type=jnp.float32
            ).reshape(COMP, members, seg)
            if role != 1:
                inside = (limits[slot, 0] < j) & (limits[slot, 1] >= j)
                turned = jnp.where(inside[None], turned, 0.0)
            orb[slot, j] = turned.astype(jnp.bfloat16)

        @pl.loop(0, depth, unroll=8)
        def _(z):
            x = got[role, :, z + 1].reshape(members * COMP, seg)
            fine = jnp.dot(
                order_ref[members * COMP :], x, preferred_element_type=jnp.float32
            ).reshape(COMP, members, seg)
            hx = got_halo[role, :, z].reshape(members * COMP // 2, 128)
            edge = jnp.dot(pick_ref[...], hx, preferred_element_type=jnp.float32)
            edge = jnp.where(keep, edge, 0.0).astype(jnp.bfloat16)
            here = orb[slot, z + 1].reshape(members * COMP, seg)
            term = jnp.dot(here, lap_ref[:seg], preferred_element_type=jnp.float32)
            term += jnp.dot(edge, lap_ref[seg:], preferred_element_type=jnp.float32)
            term = term.reshape(COMP, members, seg)
            pot = got_pot[z].astype(jnp.float32)
            vals = [fine[k] * pot[k : k + 1] for k in range(COMP)]
            width = 1
            while width < COMP:
                vals = [
                    vals[k] + vals[k + width] if not k & width else vals[k - width] - vals[k]
                    for k in range(COMP)
                ]
                width *= 2
            inside = (limits[slot, 0] <= z) & (limits[slot, 1] > z)
            for c in range(COMP):
                beside = orb[slot, z, c].astype(jnp.float32) + orb[slot, z + 2, c].astype(
                    jnp.float32
                )
                total = term[c] - 0.5 * beside + vals[c] * (1.0 / COMP)
                app[slot, z, c] = jnp.where(inside, total, 0.0).astype(jnp.bfloat16)

    def gram(z, acc):
        for c in range(COMP):
            columns = jnp.concatenate([orb[k, z + 1, c] for k in range(3)], 0)
            images = jnp.concatenate([app[k, z, c] for k in range(3)], 0)
            acc += lax.dot_general(
                jnp.concatenate([columns, images], 0),
                columns,
                (((1,), (1,)), ((), ())),
                preferred_element_type=jnp.float32,
            )
        return acc

    wide = 3 * members
    rows[...] = jnp.zeros_like(rows)
    acc = lax.fori_loop(0, depth, gram, jnp.zeros((2 * wide, wide), jnp.float32), unroll=4)
    for slot in range(3):
        for g in range(groups):
            at = slot * members + g * per
            rows[slot, g, 0:per, 0:wide] = acc[at : at + per]
            rows[slot, g, per : 2 * per, 0:wide] = acc[wide + at : wide + at + per]

    for step, to in enumerate(targets):
        for role in (2, 1, 0):
            slot = slots[role]
            move(
                role,
                step,
                rows.at[slot, to],
                got_rows.at[slot, me],
                send_rows,
                recv_rows.at[role, me],
                (rows_to[role], to),
            )
    for role in range(3):
        for g in range(groups):
            block = got_rows.at[slots[role], g]
            pltpu.make_async_copy(block, block, recv_rows.at[role, g]).wait()
    parts = []
    for slot in range(3):
        part = got_rows[slot, 0]
        for g in range(1, groups):
            part = part + got_rows[slot, g]
        parts.append(part)
    out_ref[...] = (
        pltpu.roll(parts[0], 2 * members, 1) + pltpu.roll(parts[1], members, 1) + parts[2]
    )
    pot_copy.wait_send()
    for copy in unsent:
        copy.wait_send()


def split_kernel(band_ref, margin_ref, ham_ref):
    per, width = margin_ref.shape
    margin_ref[...] = band_ref[:per, :width]
    ham_ref[...] = band_ref[per:, :width]


def local(slabs, groups, potential, coefficients, box_center, box_extent):
    per, box, comp, cells = coefficients.shape
    depth = potential.shape[0]
    members = groups * per
    seg = cells // groups
    vmem = pl.BlockSpec(memory_space=pltpu.VMEM)
    smem = pl.BlockSpec(memory_space=pltpu.SMEM)
    anywhere = pl.BlockSpec(memory_space=pl.ANY)
    frames = lambda n: pltpu.VMEM((n, groups, depth + 2, per * comp, seg), jnp.bfloat16)
    halos = lambda n: pltpu.VMEM((n, groups, depth, per * comp // 2, 128), jnp.bfloat16)
    sums = pltpu.VMEM((3, groups, 2 * per, 128), jnp.float32)
    dma = pltpu.SemaphoreType.DMA
    band = pl.pallas_call(
        functools.partial(band_kernel, slabs, groups, depth),
        out_shape=jax.ShapeDtypeStruct((2 * per, 128), jnp.float32),
        in_specs=[vmem, anywhere, smem, smem, vmem, vmem, vmem],
        out_specs=vmem,
        scratch_shapes=[
            frames(2),
            halos(2),
            frames(3),
            halos(3),
            pltpu.VMEM((depth, comp, seg), jnp.bfloat16),
            pltpu.VMEM((3, depth + 2, comp, members, seg), jnp.bfloat16),
            pltpu.VMEM((3, depth, comp, members, seg), jnp.bfloat16),
            pltpu.VMEM((3, 2, members, seg), jnp.int32),
            sums,
            sums,
            dma((3, groups)),
            dma((3, groups)),
            dma,
            dma((3, groups)),
            dma((3, groups)),
            dma((3, groups)),
            dma,
            dma((3, groups)),
        ],
        compiler_params=pltpu.CompilerParams(collective_id=0, has_side_effects=True),
        name="band",
    )(coefficients, potential, box_center, box_extent, *matrices(members, per, seg))
    out = jax.ShapeDtypeStruct((per, 5 * members), jnp.float32)
    return pl.pallas_call(
        split_kernel, out_shape=(out, out), in_specs=[vmem], out_specs=(vmem, vmem), name="split"
    )(band)


def solution(mesh):
    return jax.shard_map(
        functools.partial(local, mesh.shape["slab"], mesh.shape["grp"]),
        mesh=mesh,
        in_specs=(P("slab", None, None), P(("slab", "grp"), None, None, None), P(), P()),
        out_specs=(P(("slab", "grp"), None), P(("slab", "grp"), None)),
        check_vma=False,
    )
```

profile of v0, /device:TPU:0, one launch (start us, length us, event | category | flops | bytes accessed | tf_op | source)
XLA Modules:
  0.0 38.3 jit_solution(10147486404590187881)
XLA Ops:
  0.6 36.4 %band.1.band_ref = f32[8,128]{1,0:T(8,128)} custom-call(bf16[4,16,8,1024]{3,2,1,0:T(8,128)(2,1)} %coef_ref.1, bf16[8,8,1024]{2,1,0:T(8,128)(2,1)} %pot_ref.1, s32[128]{0:T(128)} %center_ref.1, s32[128]{0:T(128)} %extent_ref.1, bf16[256,128]{1,0:T(8,128)(2,1)} %constant.6.clone.order_ref, bf16[128,64]{1,0:T(8,128)(2,1)} %constant.7.clone.pick_ref, ...), custom_call_target="tpu_custom_call" | custom-call | tf_op jit(solution)/shard_map/band/pallas_call | solution.py:377
  37.0 1.3 %split.1 = (f32[4,80]{1,0:T(4,128)}, f32[4,80]{1,0:T(4,128)}) custom-call(f32[8,128]{1,0:T(8,128)} %band.1.band_ref), custom_call_target="tpu_custom_call" | custom-call | tf_op jit(solution)/shard_map/split/pallas_call | solution.py:406
where the time goes:
time: 38.5 us; the launch traced here: 38.3 us
  Pallas kernels  37.7 us (98%)
  between operations  0.64 us (2%)
    pallas_call x1, Pallas kernels, local(): pl.pallas_call(functools.partial(band_kernel, slabs, groups, depth), out_...  36.4 us
    pallas_call x1, Pallas kernels, local(): pl.pallas_call(split_kernel, out_shape=(out, out), in_specs=[vmem], out_s...  1.27 us

commit v1 on v0

v1 whole, which is shorter than its diff:
```python
import functools

import jax
import jax.numpy as jnp
import numpy as np
from jax import lax
from jax.experimental import pallas as pl
from jax.experimental.pallas import tpu as pltpu
from jax.sharding import PartitionSpec as P

COMP = 8
CX = 32
CY = 32
BLOCK = 256
LANES = 128
MESH = pl.DeviceIdType.MESH
PAIRS = ((0, 3), (1, 2))
SHORT = (0, 3, 1, 2)


def haar_signs():
    ids = np.arange(COMP)
    common = ids[:, None] & ids[None, :]
    parity = (common % 2 + common // 2 % 2 + common // 4 % 2) % 2
    return (1 - 2 * parity).astype(np.float32)


def matrices(rows):
    haar = np.einsum("kc,mn->kmnc", haar_signs(), np.eye(rows, dtype=np.float32))
    haar = haar.reshape(COMP * rows, rows * COMP)
    lap = np.zeros((BLOCK, BLOCK), np.float32)
    for i in range(BLOCK):
        if i % CY:
            lap[i - 1, i] = lap[i, i - 1] = -0.5
        if i >= CY:
            lap[i - CY, i] = lap[i, i - CY] = -0.5
    return jnp.asarray(haar, jnp.bfloat16), jnp.asarray(lap, jnp.bfloat16)


def band_kernel(
    slabs,
    groups,
    depth,
    pot_ref,
    center_ref,
    extent_ref,
    haar_ref,
    lap_ref,
    coef_hbm,
    out_ref,
    coef,
    frames,
    raw,
    far,
    orb,
    rest,
    pot,
    pot_out,
    pot_in,
    limits,
    acc,
    place,
    rows,
    got_rows,
    load_sem,
    pot_send,
    pot_recv,
    tile_send,
    tile_recv,
    far_send,
    far_recv,
    rows_send,
    rows_recv,
):
    f32, bf16 = jnp.float32, jnp.bfloat16
    slab = lax.axis_index("slab")
    me = lax.axis_index("grp")
    per, box, comp, cells = coef.shape
    half = depth // 2
    team = 2 * groups
    rows_tile = 4 * per
    odd = lax.rem(slab, 2)
    base = slab - odd
    mine = odd * groups + me
    ahead = lax.rem(slab + 2, slabs)
    behind = lax.rem(slab + slabs - 2, slabs)

    def mate(step):
        low, scale, rest_of, bits = 0, 1, me, step
        while scale < groups:
            bit = lax.rem(rest_of, 2)
            rest_of = rest_of // 2
            low = low + scale * (1 - bit if bits % 2 else bit)
            bits //= 2
            scale *= 2
        par = 1 - odd if bits else odd
        return par, low

    steps = [6, 2, 4, 7, 3, 5, 1, 0] if groups == 4 else list(range(team - 1, -1, -1))

    loads = [
        pltpu.make_async_copy(coef_hbm.at[f], coef.at[f], load_sem.at[f]) for f in range(per)
    ]
    for copy in loads:
        copy.start()

    barrier = pltpu.get_barrier_semaphore()
    for step in steps:
        if step:
            par, low = mate(step)
            pl.semaphore_signal(
                barrier, inc=1, device_id=(base + par, low), device_id_type=MESH
            )
    for place_at in (ahead, behind):
        pl.semaphore_signal(barrier, inc=1, device_id=(place_at, me), device_id_type=MESH)

    unsent = []

    def push(source, target, send, recv, to):
        copy = pltpu.make_async_remote_copy(
            src_ref=source,
            dst_ref=target,
            send_sem=send,
            recv_sem=recv,
            device_id=to,
            device_id_type=MESH,
        )
        copy.start()
        unsent.append(copy)
        return copy

    def arrive(block, sem):
        pltpu.make_async_copy(block, block, sem).wait()

    def iota(shape, dim):
        return lax.broadcasted_iota(jnp.int32, shape, dim)

    def plane_of(row):
        pair = row // 8
        first = jnp.where(pair == 1, 3, jnp.where(pair == 2, 1, jnp.where(pair == 3, 2, 0)))
        return first + half * (lax.rem(row, 8) // per)

    theirs = (1 - odd) * groups + me
    own_pot = pot_ref[...].astype(f32).reshape(depth * comp, cells).astype(bf16)
    at_plane, at_column = iota((16, depth * comp), 0), iota((16, depth * comp), 1)
    pick = jnp.where(at_column == at_plane * comp + theirs, 1.0, 0.0).astype(bf16)
    sent = jnp.dot(pick, own_pot, preferred_element_type=f32)
    pot_out[...] = sent[:depth].astype(bf16)
    at_row, at_column = iota((4 * depth, depth * comp), 0), iota((4 * depth, depth * comp), 1)
    pick = jnp.where(at_column == plane_of(at_row) * comp + mine, 1.0, 0.0).astype(bf16)
    pot[odd] = jnp.dot(pick, own_pot, preferred_element_type=f32)

    row8 = iota((8, LANES), 0)
    func = lax.rem(row8, per)
    upper = row8 // per

    def spread(values):
        vec = jnp.full((8, LANES), values[0], jnp.int32)
        for f in range(1, per):
            vec = jnp.where(func == f, values[f], vec)
        return vec

    first = (slab * groups + me) * per
    extents = [extent_ref[first + f] for f in range(per)]
    starts = [
        center_ref[first + f] - slab * depth - lax.shift_right_logical(extents[f], 1)
        for f in range(per)
    ]
    start_rows, end_rows = spread(starts), spread([s + e for s, e in zip(starts, extents)])

    def build(index, outer, pairs):
        planes, masks = [], []
        for i in pairs:
            for h in range(2):
                for f in range(per):
                    j = i + half * h
                    if outer:
                        p = j + depth - starts[f]
                        p = jnp.where(p < extents[f], p, p - 2 * depth)
                    else:
                        p = j - starts[f]
                    planes.append(coef[f, jnp.clip(p, 0, box - 1)].astype(f32))
            j = i + half * upper
            if outer:
                masks.append((j < end_rows - depth) | (j >= start_rows + depth))
            else:
                masks.append((j >= start_rows) & (j < end_rows))
        stacked = jnp.concatenate(planes, 0).astype(bf16)
        fine = jnp.dot(haar_ref[...], stacked, preferred_element_type=f32)
        keep = jnp.concatenate(masks, 0)
        for k in range(comp):
            for v in range(cells // LANES):
                at = slice(v * LANES, (v + 1) * LANES)
                part = fine[k * rows_tile : (k + 1) * rows_tile, at]
                frames[index, k, :, at] = jnp.where(keep, part, 0.0).astype(bf16)

    def tile_target(index, par, low):
        if index in (0, 3):
            return orb.at[par, index // 3, (1 + par) * groups + low]
        return raw.at[index - 1, par * groups + low]

    def send_tiles(index):
        for step in steps:
            par, low = mate(step)
            source = frames.at[index, par * groups + low]
            target = tile_target(index, odd, me)
            recv = tile_recv.at[index, mine]
            if step:
                push(source, target, tile_send.at[index, step], recv, (base + par, low))
            else:
                pltpu.make_async_copy(source, target, recv).start()

    pl.semaphore_wait(barrier, team + 1)
    push(pot_out, pot_in, pot_send, pot_recv, (base + 1 - odd, me))
    for copy in loads:
        copy.wait()
    build(0, False, PAIRS[0])
    send_tiles(0)
    build(1, True, PAIRS[0])
    send_tiles(1)
    build(2, True, PAIRS[1])
    send_tiles(2)
    build(3, False, PAIRS[1])
    send_tiles(3)

    for slot in range(4):
        home = lax.rem(base + slabs - 1 + slot, slabs)
        for g in range(groups):
            at = (home * groups + g) * per
            ext = [extent_ref[at + f] for f in range(per)]
            begin = [
                center_ref[at + f] - home * depth - lax.shift_right_logical(ext[f], 1)
                for f in range(per)
            ]
            limits[slot, g, 0] = spread(begin)
            limits[slot, g, 1] = spread([b + e for b, e in zip(begin, ext)])

    at_row, at_column = iota((2 * LANES, LANES), 0), iota((2 * LANES, LANES), 1)
    lane = lax.rem(at_row, LANES)
    slot_of = lane // 64 + 2 * (lax.rem(lane, 8 * 2) // 8)
    member = lax.rem(lane, 64) // 16 * per + lax.rem(lane, 8)
    near = at_row < LANES
    band = jnp.where(near, slot_of + 1 - odd, slot_of - 1 + 3 * odd)
    fits = (lax.rem(lane, 8) < per) & (band >= 0) & (band < 5)
    fits = fits & (at_column == band * groups * per + member)
    place[...] = jnp.where(fits, 1.0, 0.0)

    arrive(pot_in, pot_recv)
    padded = jnp.concatenate([pot_in[...].astype(f32), jnp.zeros((depth, cells), f32)], 0)
    at_row, at_column = iota((4 * depth, 2 * depth), 0), iota((4 * depth, 2 * depth), 1)
    pick = jnp.where(at_column == plane_of(at_row), 1.0, 0.0).astype(bf16)
    pot[1 - odd] = jnp.dot(pick, padded.astype(bf16), preferred_element_type=f32)

    for index in range(3):
        for step in steps:
            par, low = mate(step)
            block = tile_target(index, par, low)
            arrive(block, tile_recv.at[index, par * groups + low])
            to = lax.rem(slab + slabs + 4 * par - 2, slabs)
            push(
                block,
                far.at[1 - par, index, low],
                far_send.at[index, step],
                far_recv.at[1 - par, index, low],
                (to, me),
            )

    low_half = row8 < per
    lane8 = iota((8, LANES), 1)
    vregs = cells // LANES
    blocks = cells // BLOCK
    per_block = BLOCK // LANES

    def load(ref, top):
        wide = ref[top : top + 8].astype(f32)
        return [wide[:, v * LANES : (v + 1) * LANES] for v in range(vregs)]

    def swap(low_rows, high_rows):
        return [
            pltpu.roll(jnp.where(low_half, a, b), per, 0) for a, b in zip(low_rows, high_rows)
        ]

    def select(keep, rows_in):
        return [jnp.where(keep, x, 0.0) for x in rows_in]

    def split(ref):
        wide = ref[...].astype(f32)
        cut = lambda part: [part[:, v * LANES : (v + 1) * LANES] for v in range(vregs)]
        return cut(wide[:8]), cut(wide[8:])

    def finish(side, at, planes, before, after, keeps):
        tiles = [orb.at[side, t, at] for t in range(2)]
        stack = []
        for q in range(blocks):
            for t in range(2):
                stack.append(tiles[t][:, q * BLOCK : (q + 1) * BLOCK])
        beside = jnp.dot(jnp.concatenate(stack, 0), lap_ref[...], preferred_element_type=f32)
        shifted = [before, *planes, after]
        for v in range(vregs):
            done = {}
            q, part = divmod(v, per_block)
            for n, i in enumerate(SHORT):
                total = shifted[i][v] + shifted[i + 2][v]
                if part == 0 and v:
                    moved = pltpu.roll(planes[i][v - 1], CY, 1)
                    total = total + jnp.where(lane8 < CY, moved, 0.0)
                if part == per_block - 1 and v < vregs - 1:
                    moved = pltpu.roll(planes[i][v + 1], LANES - CY, 1)
                    total = total + jnp.where(lane8 >= LANES - CY, moved, 0.0)
                top = (q * 4 + n) * 8
                value = beside[top : top + 8, part * LANES : (part + 1) * LANES]
                value = value - 0.5 * total
                value = value + pot[side, n * 8 : n * 8 + 8, v * LANES : (v + 1) * LANES] * (
                    planes[i][v]
                )
                done[i] = jnp.where(keeps[i], value, 0.0)
            for t in range(2):
                both = jnp.concatenate([done[i] for i in PAIRS[t]], 0)
                rest[side, t, at, :, v * LANES : (v + 1) * LANES] = both.astype(bf16)

    def outer_frame(side, at, slot, g, up, main_tile, first_tile, second_tile):
        begin, end = limits[slot, g, 0], limits[slot, g, 1]
        if up:
            keeps = [i + half * upper < end - depth for i in range(half)]
        else:
            keeps = [i + half * upper >= begin + depth for i in range(half)]
        p0, p3 = split(first_tile)
        p1, p2 = split(second_tile)
        planes = [select(keeps[i], p) for i, p in enumerate((p0, p1, p2, p3))]
        for v in range(vregs):
            for t in range(2):
                both = jnp.concatenate([planes[i][v] for i in PAIRS[t]], 0)
                orb[side, t, at, :, v * LANES : (v + 1) * LANES] = both.astype(bf16)
        main0, main3 = split(main_tile)
        zero = [jnp.zeros((8, LANES), f32)] * vregs
        if up:
            before, after = swap(planes[3], main3), swap(zero, planes[0])
        else:
            before, after = swap(planes[3], zero), swap(main0, planes[0])
        finish(side, at, planes, before, after, keeps)

    def main_frame(side, at, slot, g, outer_tile):
        begin, end = limits[slot, g, 0], limits[slot, g, 1]
        keeps = [
            (i + half * upper >= begin) & (i + half * upper < end) for i in range(half)
        ]
        p0, p3 = split(orb.at[side, 0, at])
        p1, p2 = split(orb.at[side, 1, at])
        planes = [p0, p1, p2, p3]
        out0, out3 = split(outer_tile)
        down3 = select(half - 1 + half * upper >= begin + depth, out3)
        up0 = select(half * upper < end - depth, out0)
        finish(side, at, planes, swap(p3, down3), swap(up0, p0), keeps)

    @pl.loop(0, groups)
    def _(g):
        outer_frame(
            1, groups + g, 1, g, True, orb.at[0, 0, groups + g], raw.at[0, g], raw.at[1, g]
        )
        outer_frame(
            0,
            2 * groups + g,
            2,
            g,
            False,
            orb.at[1, 0, 2 * groups + g],
            raw.at[0, groups + g],
            raw.at[1, groups + g],
        )

    for index in range(3):
        for side in range(2):
            for g in range(groups):
                arrive(far.at[side, index, g], far_recv.at[side, index, g])

    @pl.loop(0, groups)
    def _(g):
        outer_frame(0, g, 0, g, True, far.at[0, 0, g], far.at[0, 1, g], far.at[0, 2, g])
        outer_frame(1, g, 3, g, False, far.at[1, 0, g], far.at[1, 1, g], far.at[1, 2, g])

    for step in steps:
        par, low = mate(step)
        arrive(tile_target(3, par, low), tile_recv.at[3, par * groups + low])

    @pl.loop(0, groups)
    def _(g):
        main_frame(0, groups + g, 1, g, raw.at[0, g])
        main_frame(1, 2 * groups + g, 2, g, raw.at[0, groups + g])

    count = 3 * groups
    wide = count * rows_tile
    for side in range(2):
        for t in range(2):
            columns = orb[side, t].reshape(wide, cells)
            images = rest[side, t].reshape(wide, cells)
            full = jnp.concatenate([columns, columns[: 2 * LANES - wide]], 0)
            part = lax.dot_general(
                jnp.concatenate([columns, images], 0),
                full,
                (((1,), (1,)), ((), ())),
                preferred_element_type=f32,
            )
            if t:
                acc[side] += part
            else:
                acc[side] = part

    quarter = lax.rem(lane8, 16) // per
    own_plane = [quarter == upper + 2 * pi for pi in range(2)]

    def gathered(side, at):
        both = []
        for kind in range(2):
            top = (kind * count + at) * rows_tile
            parts = []
            for v in range(2):
                lanes = slice(v * LANES, (v + 1) * LANES)
                value = jnp.where(own_plane[0], acc[side, top : top + 8, lanes], 0.0)
                value += jnp.where(own_plane[1], acc[side, top + 8 : top + 16, lanes], 0.0)
                value += pltpu.roll(value, per, 0)
                value += pltpu.roll(value, LANES - 4, 1)
                value += pltpu.roll(value, LANES - 8, 1)
                parts.append(value)
            both.append(parts)
        return [jnp.where(low_half, both[0][v], both[1][v]) for v in range(2)]

    left = lane8 < LANES // 2
    even = lax.rem(lane8, 16) < 8
    zero = jnp.zeros((8, LANES), f32)
    for slot in (3, 0, 1, 2):
        for g in range(groups):
            v0, v1 = gathered(0, slot * groups + g) if slot < 3 else (zero, zero)
            w0, w1 = gathered(1, slot % 3 * groups + g) if slot else (zero, zero)
            near_cols = jnp.where(left, v0, v0 + w0)
            far_cols = jnp.where(left, v1 + w1, pltpu.roll(w0, LANES // 2, 1))
            if slot == 3:
                near_cols = jnp.where(left, 0.0, w0)
            rows[slot, g] = jnp.where(even, near_cols, pltpu.roll(far_cols, 8, 1))

    for slot in (3, 0):
        to = lax.rem(base + slabs - 1 + slot, slabs)
        for g in range(groups):
            push(
                rows.at[slot, g],
                got_rows.at[1, mine],
                rows_send.at[slot, g],
                rows_recv.at[1, mine],
                (to, g),
            )
    for step in steps:
        par, low = mate(step)
        source, target = rows.at[1 + par, low], got_rows.at[0, mine]
        if step:
            push(source, target, rows_send.at[1, step], rows_recv.at[0, mine], (base + par, low))
        else:
            pltpu.make_async_copy(source, target, rows_recv.at[0, mine]).start()
    for side in range(2):
        for r in range(team):
            arrive(got_rows.at[side, r], rows_recv.at[side, r])
    sums = []
    for side in range(2):
        total = got_rows[side, 0]
        for r in range(1, team):
            total = total + got_rows[side, r]
        sums.append(total)
    total = jnp.dot(
        jnp.concatenate(sums, 1),
        place[...],
        preferred_element_type=f32,
        precision=lax.Precision.HIGHEST,
    ) * (1.0 / comp)
    out_ref[...] = total + jnp.where(low_half, 0.0, 3.0 * pltpu.roll(total, per, 0))
    for copy in unsent:
        copy.wait_send()


def split_kernel(band_ref, margin_ref, ham_ref):
    per, width = margin_ref.shape
    margin_ref[...] = band_ref[:per, :width]
    ham_ref[...] = band_ref[per:, :width]


def local(slabs, groups, potential, coefficients, box_center, box_extent):
    per, box, comp, cells = coefficients.shape
    depth = potential.shape[0]
    team = 2 * groups
    rows_tile = 4 * per
    assert (depth, per, comp, groups) == (8, 4, team, 4)
    vmem = pl.BlockSpec(memory_space=pltpu.VMEM)
    smem = pl.BlockSpec(memory_space=pltpu.SMEM)
    anywhere = pl.BlockSpec(memory_space=pl.ANY)
    bf16, f32 = jnp.bfloat16, jnp.float32
    tiles = lambda *lead: pltpu.VMEM((*lead, rows_tile, cells), bf16)
    dma = pltpu.SemaphoreType.DMA
    band = pl.pallas_call(
        functools.partial(band_kernel, slabs, groups, depth),
        out_shape=jax.ShapeDtypeStruct((2 * per, LANES), f32),
        in_specs=[vmem, smem, smem, vmem, vmem, anywhere],
        out_specs=vmem,
        scratch_shapes=[
            pltpu.VMEM((per, box, comp, cells), bf16),
            tiles(4, comp),
            tiles(2, team),
            tiles(2, 3, groups),
            tiles(2, 2, 3 * groups),
            tiles(2, 2, 3 * groups),
            pltpu.VMEM((2, 4 * depth, cells), f32),
            pltpu.VMEM((depth, cells), bf16),
            pltpu.VMEM((depth, cells), bf16),
            pltpu.VMEM((4, groups, 2, 8, LANES), jnp.int32),
            pltpu.VMEM((2, 6 * groups * rows_tile, 2 * LANES), f32),
            pltpu.VMEM((2 * LANES, LANES), f32),
            pltpu.VMEM((4, groups, 2 * per, LANES), f32),
            pltpu.VMEM((2, team, 2 * per, LANES), f32),
            dma((per,)),
            dma,
            dma,
            dma((4, team)),
            dma((4, team)),
            dma((3, team)),
            dma((2, 3, groups)),
            dma((4, team)),
            dma((2, team)),
        ],
        compiler_params=pltpu.CompilerParams(collective_id=0, has_side_effects=True),
        name="band",
    )(potential, box_center, box_extent, *matrices(rows_tile), coefficients)
    out = jax.ShapeDtypeStruct((per, 5 * groups * per), f32)
    return pl.pallas_call(
        split_kernel, out_shape=(out, out), in_specs=[vmem], out_specs=(vmem, vmem), name="split"
    )(band)


def solution(mesh):
    return jax.shard_map(
        functools.partial(local, mesh.shape["slab"], mesh.shape["grp"]),
        mesh=mesh,
        in_specs=(P("slab", None, None), P(("slab", "grp"), None, None, None), P(), P()),
        out_specs=(P(("slab", "grp"), None), P(("slab", "grp"), None)),
        check_vma=False,
    )
```

time: 38.5 us -> 41.4 us (1.075)
  Pallas kernels: 37.7 us -> 40.5 us
    pallas_call x1, Pallas kernels: 36.4 us -> 39.3 us  [local(): pl.pallas_call(functools.partial(band_kernel, slabs, groups, depth), out_...]
where the time goes in v1:
time: 41.4 us; the launch traced here: 41.2 us
  Pallas kernels  40.5 us (98%)
  between operations  0.64 us (2%)
    pallas_call x1, Pallas kernels, local(): pl.pallas_call(functools.partial(band_kernel, slabs, groups, depth), out_...  39.3 us
    pallas_call x1, Pallas kernels, local(): pl.pallas_call(split_kernel, out_shape=(out, out), in_specs=[vmem], out_s...  1.27 us

profile of v1, /device:TPU:0, one launch (start us, length us, event | category | flops | bytes accessed | tf_op | source)
XLA Modules:
  0.0 41.2 jit_solution(11799834923731607887)
XLA Ops:
  0.6 39.3 %band.1.band_ref = f32[8,128]{1,0:T(8,128)} custom-call(bf16[8,8,1024]{2,1,0:T(8,128)(2,1)} %pot_ref.1, s32[128]{0:T(128)} %center_ref.1, s32[128]{0:T(128)} %extent_ref.1, bf16[128,128]{1,0:T(8,128)(2,1)} %constant.4.clone.haar_ref, bf16[256,256]{1,0:T(8,128)(2,1)} %constant.5.clone.lap_ref, bf16[4,16,8,1024]{3,2,1,0:T(8,128)(2,1)} %coef_hbm.1), custom_call_target="tpu_custom_call" | custom-call | tf_op jit(solution)/shard_map/band/pallas_call | solution.py:495
  39.9 1.3 %split.1 = (f32[4,80]{1,0:T(4,128)}, f32[4,80]{1,0:T(4,128)}) custom-call(f32[8,128]{1,0:T(8,128)} %band.1.band_ref), custom_call_target="tpu_custom_call" | custom-call | tf_op jit(solution)/shard_map/split/pallas_call | solution.py:529

commit v2 on v1

--- a/solution.py
+++ b/solution.py
@@ -41,17 +41,24 @@
     slabs,
     groups,
     depth,
+    pot_hbm,
+    center_hbm,
+    extent_hbm,
+    haar_hbm,
+    lap_hbm,
+    coef_hbm,
+    out_ref,
     pot_ref,
     center_ref,
     extent_ref,
     haar_ref,
     lap_ref,
-    coef_hbm,
-    out_ref,
     coef,
     frames,
     raw,
     far,
+    halo_out,
+    halo_in,
     orb,
     rest,
     pot,
@@ -69,6 +76,8 @@
     tile_recv,
     far_send,
     far_recv,
+    halo_send,
+    halo_recv,
     rows_send,
     rows_recv,
 ):
@@ -96,10 +105,20 @@
         par = 1 - odd if bits else odd
         return par, low
 
-    steps = [6, 2, 4, 7, 3, 5, 1, 0] if groups == 4 else list(range(team - 1, -1, -1))
+    steps = [6, 2, 4, 7, 3, 5, 1, 0]
 
     loads = [
-        pltpu.make_async_copy(coef_hbm.at[f], coef.at[f], load_sem.at[f]) for f in range(per)
+        pltpu.make_async_copy(source, target, load_sem.at[n])
+        for n, (source, target) in enumerate(
+            (
+                (center_hbm, center_ref),
+                (extent_hbm, extent_ref),
+                (coef_hbm, coef),
+                (haar_hbm, haar_ref),
+                (pot_hbm, pot_ref),
+                (lap_hbm, lap_ref),
+            )
+        )
     ]
     for copy in loads:
         copy.start()
@@ -140,16 +159,6 @@
         first = jnp.where(pair == 1, 3, jnp.where(pair == 2, 1, jnp.where(pair == 3, 2, 0)))
         return first + half * (lax.rem(row, 8) // per)
 
-    theirs = (1 - odd) * groups + me
-    own_pot = pot_ref[...].astype(f32).reshape(depth * comp, cells).astype(bf16)
-    at_plane, at_column = iota((16, depth * comp), 0), iota((16, depth * comp), 1)
-    pick = jnp.where(at_column == at_plane * comp + theirs, 1.0, 0.0).astype(bf16)
-    sent = jnp.dot(pick, own_pot, preferred_element_type=f32)
-    pot_out[...] = sent[:depth].astype(bf16)
-    at_row, at_column = iota((4 * depth, depth * comp), 0), iota((4 * depth, depth * comp), 1)
-    pick = jnp.where(at_column == plane_of(at_row) * comp + mine, 1.0, 0.0).astype(bf16)
-    pot[odd] = jnp.dot(pick, own_pot, preferred_element_type=f32)
-
     row8 = iota((8, LANES), 0)
     func = lax.rem(row8, per)
     upper = row8 // per
@@ -160,6 +169,8 @@
             vec = jnp.where(func == f, values[f], vec)
         return vec
 
+    loads[0].wait()
+    loads[1].wait()
     first = (slab * groups + me) * per
     extents = [extent_ref[first + f] for f in range(per)]
     starts = [
@@ -210,18 +221,48 @@
             else:
                 pltpu.make_async_copy(source, target, recv).start()
 
+    def relay(index, step):
+        par, low = mate(step)
+        if step:
+            block = tile_target(index, par, low)
+            arrive(block, tile_recv.at[index, par * groups + low])
+        else:
+            block = frames.at[index, mine]
+        push(
+            block,
+            far.at[1 - par, index - 1, low],
+            far_send.at[index - 1, step],
+            far_recv.at[1 - par, index - 1, low],
+            (lax.rem(slab + slabs + 4 * par - 2, slabs), me),
+        )
+
+    loads[2].wait()
+    loads[3].wait()
+    build(1, True, PAIRS[0])
+    build(2, True, PAIRS[1])
     pl.semaphore_wait(barrier, team + 1)
-    push(pot_out, pot_in, pot_send, pot_recv, (base + 1 - odd, me))
-    for copy in loads:
-        copy.wait()
+    send_tiles(1)
+    relay(1, 0)
+    relay(2, 0)
     build(0, False, PAIRS[0])
     send_tiles(0)
-    build(1, True, PAIRS[0])
-    send_tiles(1)
-    build(2, True, PAIRS[1])
     send_tiles(2)
+    relay(1, 1)
     build(3, False, PAIRS[1])
     send_tiles(3)
+    relay(2, 1)
+    loads[4].wait()
+    theirs = (1 - odd) * groups + me
+    own_pot = pot_ref[...].astype(f32).reshape(depth * comp, cells).astype(bf16)
+    at_plane, at_column = iota((16, depth * comp), 0), iota((16, depth * comp), 1)
+    pick = jnp.where(at_column == at_plane * comp + theirs, 1.0, 0.0).astype(bf16)
+    sent = jnp.dot(pick, own_pot, preferred_element_type=f32)
+    pot_out[...] = sent[:depth].astype(bf16)
+    at_row, at_column = iota((4 * depth, depth * comp), 0), iota((4 * depth, depth * comp), 1)
+    pick = jnp.where(at_column == plane_of(at_row) * comp + mine, 1.0, 0.0).astype(bf16)
+    pot[odd] = jnp.dot(pick, own_pot, preferred_element_type=f32)
+
+    push(pot_out, pot_in, pot_send, pot_recv, (base + 1 - odd, me))
 
     for slot in range(4):
         home = lax.rem(base + slabs - 1 + slot, slabs)
@@ -245,36 +286,50 @@
     fits = fits & (at_column == band * groups * per + member)
     place[...] = jnp.where(fits, 1.0, 0.0)
 
+    low_half = row8 < per
+    lane8 = iota((8, LANES), 1)
+    vregs = cells // LANES
+    blocks = cells // BLOCK
+    per_block = BLOCK // LANES
+
+    def split(ref):
+        wide = ref[...].astype(f32)
+        cut = lambda part: [part[:, v * LANES : (v + 1) * LANES] for v in range(vregs)]
+        return cut(wide[:8]), cut(wide[8:])
+
+    for step in steps[:6]:
+        relay(1, step)
+    for step in steps:
+        par, low = mate(step)
+        arrive(tile_target(0, par, low), tile_recv.at[0, par * groups + low])
+    for side in range(2):
+        edges = [split(orb.at[side, 0, (1 + side) * groups + g])[side] for g in range(groups)]
+        for n in range(groups // 2):
+            one, two = edges[2 * n], edges[2 * n + 1]
+            for v in range(vregs):
+                if side:
+                    both = jnp.where(low_half, pltpu.roll(one[v], per, 0), two[v])
+                else:
+                    both = jnp.where(low_half, one[v], pltpu.roll(two[v], per, 0))
+                halo_out[side, 8 * n : 8 * n + 8, v * LANES : (v + 1) * LANES] = both.astype(bf16)
+        push(
+            halo_out.at[side],
+            halo_in.at[1 - side],
+            halo_send.at[side],
+            halo_recv.at[1 - side],
+            (ahead if side else behind, me),
+        )
+    for step in steps[:6]:
+        relay(2, step)
+    for index in (1, 2):
+        arrive(tile_target(index, odd, me), tile_recv.at[index, mine])
+    loads[5].wait()
     arrive(pot_in, pot_recv)
     padded = jnp.concatenate([pot_in[...].astype(f32), jnp.zeros((depth, cells), f32)], 0)
     at_row, at_column = iota((4 * depth, 2 * depth), 0), iota((4 * depth, 2 * depth), 1)
     pick = jnp.where(at_column == plane_of(at_row), 1.0, 0.0).astype(bf16)
     pot[1 - odd] = jnp.dot(pick, padded.astype(bf16), preferred_element_type=f32)
 
-    for index in range(3):
-        for step in steps:
-            par, low = mate(step)
-            block = tile_target(index, par, low)
-            arrive(block, tile_recv.at[index, par * groups + low])
-            to = lax.rem(slab + slabs + 4 * par - 2, slabs)
-            push(
-                block,
-                far.at[1 - par, index, low],
-                far_send.at[index, step],
-                far_recv.at[1 - par, index, low],
-                (to, me),
-            )
-
-    low_half = row8 < per
-    lane8 = iota((8, LANES), 1)
-    vregs = cells // LANES
-    blocks = cells // BLOCK
-    per_block = BLOCK // LANES
-
-    def load(ref, top):
-        wide = ref[top : top + 8].astype(f32)
-        return [wide[:, v * LANES : (v + 1) * LANES] for v in range(vregs)]
-
     def swap(low_rows, high_rows):
         return [
             pltpu.roll(jnp.where(low_half, a, b), per, 0) for a, b in zip(low_rows, high_rows)
@@ -282,11 +337,6 @@
 
     def select(keep, rows_in):
         return [jnp.where(keep, x, 0.0) for x in rows_in]
-
-    def split(ref):
-        wide = ref[...].astype(f32)
-        cut = lambda part: [part[:, v * LANES : (v + 1) * LANES] for v in range(vregs)]
-        return cut(wide[:8]), cut(wide[8:])
 
     def finish(side, at, planes, before, after, keeps):
         tiles = [orb.at[side, t, at] for t in range(2)]
@@ -318,7 +368,7 @@
                 both = jnp.concatenate([done[i] for i in PAIRS[t]], 0)
                 rest[side, t, at, :, v * LANES : (v + 1) * LANES] = both.astype(bf16)
 
-    def outer_frame(side, at, slot, g, up, main_tile, first_tile, second_tile):
+    def outer_frame(side, at, slot, g, up, edge, first_tile, second_tile):
         begin, end = limits[slot, g, 0], limits[slot, g, 1]
         if up:
             keeps = [i + half * upper < end - depth for i in range(half)]
@@ -331,12 +381,11 @@
             for t in range(2):
                 both = jnp.concatenate([planes[i][v] for i in PAIRS[t]], 0)
                 orb[side, t, at, :, v * LANES : (v + 1) * LANES] = both.astype(bf16)
-        main0, main3 = split(main_tile)
         zero = [jnp.zeros((8, LANES), f32)] * vregs
         if up:
-            before, after = swap(planes[3], main3), swap(zero, planes[0])
+            before, after = swap(planes[3], edge), swap(zero, planes[0])
         else:
-            before, after = swap(planes[3], zero), swap(main0, planes[0])
+            before, after = swap(planes[3], zero), swap(edge, planes[0])
         finish(side, at, planes, before, after, keeps)
 
     def main_frame(side, at, slot, g, outer_tile):
@@ -354,29 +403,11 @@
 
     @pl.loop(0, groups)
     def _(g):
-        outer_frame(
-            1, groups + g, 1, g, True, orb.at[0, 0, groups + g], raw.at[0, g], raw.at[1, g]
-        )
-        outer_frame(
-            0,
-            2 * groups + g,
-            2,
-            g,
-            False,
-            orb.at[1, 0, 2 * groups + g],
-            raw.at[0, groups + g],
-            raw.at[1, groups + g],
-        )
-
-    for index in range(3):
-        for side in range(2):
-            for g in range(groups):
-                arrive(far.at[side, index, g], far_recv.at[side, index, g])
-
-    @pl.loop(0, groups)
-    def _(g):
-        outer_frame(0, g, 0, g, True, far.at[0, 0, g], far.at[0, 1, g], far.at[0, 2, g])
-        outer_frame(1, g, 3, g, False, far.at[1, 0, g], far.at[1, 1, g], far.at[1, 2, g])
+        edge = split(orb.at[0, 0, groups + g])[1]
+        outer_frame(1, groups + g, 1, g, True, edge, raw.at[0, g], raw.at[1, g])
+        edge = split(orb.at[1, 0, 2 * groups + g])[0]
+        theirs = groups + g
+        outer_frame(0, groups + theirs, 2, g, False, edge, raw.at[0, theirs], raw.at[1, theirs])
 
     for step in steps:
         par, low = mate(step)
@@ -386,6 +417,17 @@
     def _(g):
         main_frame(0, groups + g, 1, g, raw.at[0, g])
         main_frame(1, 2 * groups + g, 2, g, raw.at[0, groups + g])
+
+    for side in range(2):
+        arrive(halo_in.at[side], halo_recv.at[side])
+        for g in range(groups):
+            for index in range(2):
+                arrive(far.at[side, index, g], far_recv.at[side, index, g])
+            edge = split(halo_in.at[side])[g // 2]
+            if g % 2 == side:
+                edge = [pltpu.roll(x, per, 0) for x in edge]
+            slot = 3 * side
+            outer_frame(side, g, slot, g, not side, edge, far.at[side, 0, g], far.at[side, 1, g])
 
     count = 3 * groups
     wide = count * rows_tile
@@ -487,7 +529,6 @@
     rows_tile = 4 * per
     assert (depth, per, comp, groups) == (8, 4, team, 4)
     vmem = pl.BlockSpec(memory_space=pltpu.VMEM)
-    smem = pl.BlockSpec(memory_space=pltpu.SMEM)
     anywhere = pl.BlockSpec(memory_space=pl.ANY)
     bf16, f32 = jnp.bfloat16, jnp.float32
     tiles = lambda *lead: pltpu.VMEM((*lead, rows_tile, cells), bf16)
@@ -495,13 +536,20 @@
     band = pl.pallas_call(
         functools.partial(band_kernel, slabs, groups, depth),
         out_shape=jax.ShapeDtypeStruct((2 * per, LANES), f32),
-        in_specs=[vmem, smem, smem, vmem, vmem, anywhere],
+        in_specs=[anywhere] * 6,
         out_specs=vmem,
         scratch_shapes=[
+            pltpu.VMEM(potential.shape, bf16),
+            pltpu.SMEM(box_center.shape, jnp.int32),
+            pltpu.SMEM(box_extent.shape, jnp.int32),
+            pltpu.VMEM((comp * rows_tile, comp * rows_tile), bf16),
+            pltpu.VMEM((BLOCK, BLOCK), bf16),
             pltpu.VMEM((per, box, comp, cells), bf16),
             tiles(4, comp),
             tiles(2, team),
-            tiles(2, 3, groups),
+            tiles(2, 2, groups),
+            tiles(2),
+            tiles(2),
             tiles(2, 2, 3 * groups),
             tiles(2, 2, 3 * groups),
             pltpu.VMEM((2, 4 * depth, cells), f32),
@@ -512,13 +560,15 @@
             pltpu.VMEM((2 * LANES, LANES), f32),
             pltpu.VMEM((4, groups, 2 * per, LANES), f32),
             pltpu.VMEM((2, team, 2 * per, LANES), f32),
-            dma((per,)),
+            dma((6,)),
             dma,
             dma,
             dma((4, team)),
             dma((4, team)),
-            dma((3, team)),
-            dma((2, 3, groups)),
+            dma((2, team)),
+            dma((2, 2, groups)),
+            dma((2,)),
+            dma((2,)),
             dma((4, team)),
             dma((2, team)),
         ],

time: 41.4 us -> 32.1 us (0.78)
  Pallas kernels: 40.5 us -> 31.3 us
    pallas_call x1, Pallas kernels: 39.3 us -> 30 us  [local(): pl.pallas_call(functools.partial(band_kernel, slabs, groups, depth), out_...]
where the time goes in v2:
time: 32.1 us; the launch traced here: 32 us
  Pallas kernels  31.3 us (98%)
  between operations  0.64 us (2%)
    pallas_call x1, Pallas kernels, local(): pl.pallas_call(functools.partial(band_kernel, slabs, groups, depth), out_...  30 us
    pallas_call x1, Pallas kernels, local(): pl.pallas_call(split_kernel, out_shape=(out, out), in_specs=[vmem], out_s...  1.27 us

profile of v2, /device:TPU:0, one launch (start us, length us, event | category | flops | bytes accessed | tf_op | source)
XLA Modules:
  0.0 32.0 jit_solution(15374202819960980960)
XLA Ops:
  0.6 30.0 %band.1.band_ref = f32[8,128]{1,0:T(8,128)} custom-call(bf16[8,8,1024]{2,1,0:T(8,128)(2,1)} %pot_hbm.1, s32[128]{0:T(128)} %center_hbm.1, s32[128]{0:T(128)} %extent_hbm.1, bf16[128,128]{1,0:T(8,128)(2,1)} %constant.4.clone.haar_hbm, bf16[256,256]{1,0:T(8,128)(2,1)} %constant.5.clone.lap_hbm, bf16[4,16,8,1024]{3,2,1,0:T(8,128)(2,1)} %coef_hbm.1), custom_call_target="tpu_custom_call" | custom-call | tf_op jit(solution)/shard_map/band/pallas_call | solution.py:536
  30.7 1.3 %split.1 = (f32[4,80]{1,0:T(4,128)}, f32[4,80]{1,0:T(4,128)}) custom-call(f32[8,128]{1,0:T(8,128)} %band.1.band_ref), custom_call_target="tpu_custom_call" | custom-call | tf_op jit(solution)/shard_map/split/pallas_call | solution.py:579

commit v3 on v2

--- a/solution.py
+++ b/solution.py
@@ -58,7 +58,6 @@
     raw,
     far,
     halo_out,
-    halo_in,
     orb,
     rest,
     pot,
@@ -70,15 +69,11 @@
     rows,
     got_rows,
     load_sem,
-    pot_send,
+    sent_sem,
     pot_recv,
-    tile_send,
-    tile_recv,
-    far_send,
+    outer_recv,
+    main_recv,
     far_recv,
-    halo_send,
-    halo_recv,
-    rows_send,
     rows_recv,
 ):
     f32, bf16 = jnp.float32, jnp.bfloat16
@@ -133,20 +128,16 @@
     for place_at in (ahead, behind):
         pl.semaphore_signal(barrier, inc=1, device_id=(place_at, me), device_id_type=MESH)
 
-    unsent = []
-
-    def push(source, target, send, recv, to):
+    def push(kind, source, target, recv, to):
         copy = pltpu.make_async_remote_copy(
             src_ref=source,
             dst_ref=target,
-            send_sem=send,
+            send_sem=sent_sem.at[kind],
             recv_sem=recv,
             device_id=to,
             device_id_type=MESH,
         )
         copy.start()
-        unsent.append(copy)
-        return copy
 
     def arrive(block, sem):
         pltpu.make_async_copy(block, block, sem).wait()
@@ -210,48 +201,59 @@
             return orb.at[par, index // 3, (1 + par) * groups + low]
         return raw.at[index - 1, par * groups + low]
 
+    def arrive_main(index):
+        arrive(frames.at[0], main_recv.at[index])
+
     def send_tiles(index):
         for step in steps:
             par, low = mate(step)
             source = frames.at[index, par * groups + low]
             target = tile_target(index, odd, me)
-            recv = tile_recv.at[index, mine]
+            recv = main_recv.at[index // 3] if index in (0, 3) else outer_recv.at[index - 1, mine]
             if step:
-                push(source, target, tile_send.at[index, step], recv, (base + par, low))
+                push(0, source, target, recv, (base + par, low))
             else:
                 pltpu.make_async_copy(source, target, recv).start()
 
-    def relay(index, step):
-        par, low = mate(step)
-        if step:
+    urgent = base // 2 // ((slabs + 2) // 4)
+    own_first = 1 - lax.rem(urgent + odd, 2)
+
+    def relay(index, place):
+        if place < 2:
+            par, low = mate(place)
+        else:
+            own = place - 2 < 2, place - 2 >= 4
+            par = odd + (1 - 2 * odd) * (1 - (own[0] * own_first + own[1] * (1 - own_first)))
+            first = mate((2, 3, 0, 1, 2, 3)[place - 2])[1]
+            second = mate((0, 1, 2, 3, 2, 3)[place - 2])[1]
+            low = own_first * first + (1 - own_first) * second
+        if place:
             block = tile_target(index, par, low)
-            arrive(block, tile_recv.at[index, par * groups + low])
+            arrive(block, outer_recv.at[index - 1, par * groups + low])
         else:
             block = frames.at[index, mine]
         push(
+            1,
             block,
-            far.at[1 - par, index - 1, low],
-            far_send.at[index - 1, step],
-            far_recv.at[1 - par, index - 1, low],
+            far.at[1 - par, (index - 1) * groups + low],
+            far_recv.at[1 - par],
             (lax.rem(slab + slabs + 4 * par - 2, slabs), me),
         )
 
     loads[2].wait()
     loads[3].wait()
     build(1, True, PAIRS[0])
-    build(2, True, PAIRS[1])
     pl.semaphore_wait(barrier, team + 1)
     send_tiles(1)
     relay(1, 0)
+    build(2, True, PAIRS[1])
     relay(2, 0)
     build(0, False, PAIRS[0])
     send_tiles(0)
     send_tiles(2)
     relay(1, 1)
-    build(3, False, PAIRS[1])
-    send_tiles(3)
-    relay(2, 1)
     loads[4].wait()
+    loads[5].wait()
     theirs = (1 - odd) * groups + me
     own_pot = pot_ref[...].astype(f32).reshape(depth * comp, cells).astype(bf16)
     at_plane, at_column = iota((16, depth * comp), 0), iota((16, depth * comp), 1)
@@ -262,7 +264,11 @@
     pick = jnp.where(at_column == plane_of(at_row) * comp + mine, 1.0, 0.0).astype(bf16)
     pot[odd] = jnp.dot(pick, own_pot, preferred_element_type=f32)
 
-    push(pot_out, pot_in, pot_send, pot_recv, (base + 1 - odd, me))
+    push(3, pot_out, pot_in, pot_recv, (base + 1 - odd, me))
+
+    build(3, False, PAIRS[1])
+    send_tiles(3)
+    relay(2, 1)
 
     for slot in range(4):
         home = lax.rem(base + slabs - 1 + slot, slabs)
@@ -297,11 +303,9 @@
         cut = lambda part: [part[:, v * LANES : (v + 1) * LANES] for v in range(vregs)]
         return cut(wide[:8]), cut(wide[8:])
 
-    for step in steps[:6]:
-        relay(1, step)
-    for step in steps:
-        par, low = mate(step)
-        arrive(tile_target(0, par, low), tile_recv.at[0, par * groups + low])
+    for turn in range(2, 8):
+        relay(1, turn)
+    arrive_main(0)
     for side in range(2):
         edges = [split(orb.at[side, 0, (1 + side) * groups + g])[side] for g in range(groups)]
         for n in range(groups // 2):
@@ -313,17 +317,16 @@
                     both = jnp.where(low_half, one[v], pltpu.roll(two[v], per, 0))
                 halo_out[side, 8 * n : 8 * n + 8, v * LANES : (v + 1) * LANES] = both.astype(bf16)
         push(
+            2,
             halo_out.at[side],
-            halo_in.at[1 - side],
-            halo_send.at[side],
-            halo_recv.at[1 - side],
+            far.at[1 - side, 2 * groups],
+            far_recv.at[1 - side],
             (ahead if side else behind, me),
         )
-    for step in steps[:6]:
-        relay(2, step)
+    for turn in range(2, 8):
+        relay(2, turn)
     for index in (1, 2):
-        arrive(tile_target(index, odd, me), tile_recv.at[index, mine])
-    loads[5].wait()
+        arrive(tile_target(index, odd, me), outer_recv.at[index - 1, mine])
     arrive(pot_in, pot_recv)
     padded = jnp.concatenate([pot_in[...].astype(f32), jnp.zeros((depth, cells), f32)], 0)
     at_row, at_column = iota((4 * depth, 2 * depth), 0), iota((4 * depth, 2 * depth), 1)
@@ -409,44 +412,6 @@
         theirs = groups + g
         outer_frame(0, groups + theirs, 2, g, False, edge, raw.at[0, theirs], raw.at[1, theirs])
 
-    for step in steps:
-        par, low = mate(step)
-        arrive(tile_target(3, par, low), tile_recv.at[3, par * groups + low])
-
-    @pl.loop(0, groups)
-    def _(g):
-        main_frame(0, groups + g, 1, g, raw.at[0, g])
-        main_frame(1, 2 * groups + g, 2, g, raw.at[0, groups + g])
-
-    for side in range(2):
-        arrive(halo_in.at[side], halo_recv.at[side])
-        for g in range(groups):
-            for index in range(2):
-                arrive(far.at[side, index, g], far_recv.at[side, index, g])
-            edge = split(halo_in.at[side])[g // 2]
-            if g % 2 == side:
-                edge = [pltpu.roll(x, per, 0) for x in edge]
-            slot = 3 * side
-            outer_frame(side, g, slot, g, not side, edge, far.at[side, 0, g], far.at[side, 1, g])
-
-    count = 3 * groups
-    wide = count * rows_tile
-    for side in range(2):
-        for t in range(2):
-            columns = orb[side, t].reshape(wide, cells)
-            images = rest[side, t].reshape(wide, cells)
-            full = jnp.concatenate([columns, columns[: 2 * LANES - wide]], 0)
-            part = lax.dot_general(
-                jnp.concatenate([columns, images], 0),
-                full,
-                (((1,), (1,)), ((), ())),
-                preferred_element_type=f32,
-            )
-            if t:
-                acc[side] += part
-            else:
-                acc[side] = part
-
     quarter = lax.rem(lane8, 16) // per
     own_plane = [quarter == upper + 2 * pi for pi in range(2)]
 
@@ -468,42 +433,80 @@
 
     left = lane8 < LANES // 2
     even = lax.rem(lane8, 16) < 8
-    zero = jnp.zeros((8, LANES), f32)
-    for slot in (3, 0, 1, 2):
+    count = 3 * groups
+    wide = count * rows_tile
+
+    def far_side(side):
+        arrive(far.at[side], far_recv.at[side])
         for g in range(groups):
-            v0, v1 = gathered(0, slot * groups + g) if slot < 3 else (zero, zero)
-            w0, w1 = gathered(1, slot % 3 * groups + g) if slot else (zero, zero)
+            edge = split(far.at[side, 2 * groups])[g // 2]
+            if g % 2 == side:
+                edge = [pltpu.roll(x, per, 0) for x in edge]
+            outer_frame(side, g, 3 * side, g, not side, edge, far.at[side, g], far.at[side, groups + g])
+
+    def products(side):
+        for t in range(2):
+            columns = orb[side, t].reshape(wide, cells)
+            images = rest[side, t].reshape(wide, cells)
+            full = jnp.concatenate([columns, columns[: 2 * LANES - wide]], 0)
+            part = lax.dot_general(
+                jnp.concatenate([columns, images], 0),
+                full,
+                (((1,), (1,)), ((), ())),
+                preferred_element_type=f32,
+            )
+            if t:
+                acc[side] += part
+            else:
+                acc[side] = part
+        for g in range(groups):
+            one, two = gathered(side, g)
+            if side:
+                near_cols = jnp.where(left, 0.0, one)
+                far_cols = jnp.where(left, two, pltpu.roll(one, LANES // 2, 1))
+            else:
+                near_cols, far_cols = one, jnp.where(left, two, 0.0)
+            rows[3 * side, g] = jnp.where(even, near_cols, pltpu.roll(far_cols, 8, 1))
+
+    arrive_main(1)
+    @pl.loop(0, groups)
+    def _(g):
+        main_frame(0, groups + g, 1, g, raw.at[0, g])
+        main_frame(1, 2 * groups + g, 2, g, raw.at[0, groups + g])
+    for turn in range(2):
+        now = urgent + turn - 2 * urgent * turn
+        for side in range(2):
+            pl.when(now == side)(functools.partial(far_side, side))
+        for side in range(2):
+            pl.when(now == side)(functools.partial(products, side))
+        for g in range(groups):
+            push(
+                4,
+                rows.at[3 * now, g],
+                got_rows.at[team + mine],
+                rows_recv,
+                (lax.rem(base + slabs - 1 + 3 * now, slabs), g),
+            )
+    for slot in (1, 2):
+        for g in range(groups):
+            v0, v1 = gathered(0, slot * groups + g)
+            w0, w1 = gathered(1, slot * groups + g)
             near_cols = jnp.where(left, v0, v0 + w0)
             far_cols = jnp.where(left, v1 + w1, pltpu.roll(w0, LANES // 2, 1))
-            if slot == 3:
-                near_cols = jnp.where(left, 0.0, w0)
             rows[slot, g] = jnp.where(even, near_cols, pltpu.roll(far_cols, 8, 1))
-
-    for slot in (3, 0):
-        to = lax.rem(base + slabs - 1 + slot, slabs)
-        for g in range(groups):
-            push(
-                rows.at[slot, g],
-                got_rows.at[1, mine],
-                rows_send.at[slot, g],
-                rows_recv.at[1, mine],
-                (to, g),
-            )
     for step in steps:
         par, low = mate(step)
-        source, target = rows.at[1 + par, low], got_rows.at[0, mine]
+        source, target = rows.at[1 + par, low], got_rows.at[mine]
         if step:
-            push(source, target, rows_send.at[1, step], rows_recv.at[0, mine], (base + par, low))
+            push(4, source, target, rows_recv, (base + par, low))
         else:
-            pltpu.make_async_copy(source, target, rows_recv.at[0, mine]).start()
-    for side in range(2):
-        for r in range(team):
-            arrive(got_rows.at[side, r], rows_recv.at[side, r])
+            pltpu.make_async_copy(source, target, rows_recv).start()
+    arrive(got_rows, rows_recv)
     sums = []
     for side in range(2):
-        total = got_rows[side, 0]
+        total = got_rows[side * team]
         for r in range(1, team):
-            total = total + got_rows[side, r]
+            total = total + got_rows[side * team + r]
         sums.append(total)
     total = jnp.dot(
         jnp.concatenate(sums, 1),
@@ -512,8 +515,10 @@
         precision=lax.Precision.HIGHEST,
     ) * (1.0 / comp)
     out_ref[...] = total + jnp.where(low_half, 0.0, 3.0 * pltpu.roll(total, per, 0))
-    for copy in unsent:
-        copy.wait_send()
+    for kind, block in enumerate(
+        (frames.at[:, : comp - 1], raw, halo_out, pot_out, got_rows.at[: 2 * team - 1])
+    ):
+        arrive(block, sent_sem.at[kind])
 
 
 def split_kernel(band_ref, margin_ref, ham_ref):
@@ -547,8 +552,7 @@
             pltpu.VMEM((per, box, comp, cells), bf16),
             tiles(4, comp),
             tiles(2, team),
-            tiles(2, 2, groups),
-            tiles(2),
+            tiles(2, 2 * groups + 1),
             tiles(2),
             tiles(2, 2, 3 * groups),
             tiles(2, 2, 3 * groups),
@@ -559,18 +563,14 @@
             pltpu.VMEM((2, 6 * groups * rows_tile, 2 * LANES), f32),
             pltpu.VMEM((2 * LANES, LANES), f32),
             pltpu.VMEM((4, groups, 2 * per, LANES), f32),
-            pltpu.VMEM((2, team, 2 * per, LANES), f32),
+            pltpu.VMEM((2 * team, 2 * per, LANES), f32),
             dma((6,)),
+            dma((5,)),
             dma,
-            dma,
-            dma((4, team)),
-            dma((4, team)),
             dma((2, team)),
-            dma((2, 2, groups)),
             dma((2,)),
             dma((2,)),
-            dma((4, team)),
-            dma((2, team)),
+            dma,
         ],
         compiler_params=pltpu.CompilerParams(collective_id=0, has_side_effects=True),
         name="band",

time: 32.1 us -> 29.6 us (0.922)
  Pallas kernels: 31.3 us -> 28.8 us
    pallas_call x1, Pallas kernels: 30 us -> 27.5 us  [local(): pl.pallas_call(functools.partial(band_kernel, slabs, groups, depth), out_...]
where the time goes in v3:
time: 29.6 us; the launch traced here: 29.4 us
  Pallas kernels  28.8 us (97%)
  between operations  0.64 us (2%)
    pallas_call x1, Pallas kernels, local(): pl.pallas_call(functools.partial(band_kernel, slabs, groups, depth), out_...  27.5 us
    pallas_call x1, Pallas kernels, local(): pl.pallas_call(split_kernel, out_shape=(out, out), in_specs=[vmem], out_s...  1.27 us

profile of v3, /device:TPU:0, one launch (start us, length us, event | category | flops | bytes accessed | tf_op | source)
XLA Modules:
  0.0 29.4 jit_solution(14588807850073933675)
XLA Ops:
  0.6 27.5 %band.1.band_ref = f32[8,128]{1,0:T(8,128)} custom-call(bf16[8,8,1024]{2,1,0:T(8,128)(2,1)} %pot_hbm.1, s32[128]{0:T(128)} %center_hbm.1, s32[128]{0:T(128)} %extent_hbm.1, bf16[128,128]{1,0:T(8,128)(2,1)} %constant.4.clone.haar_hbm, bf16[256,256]{1,0:T(8,128)(2,1)} %constant.5.clone.lap_hbm, bf16[4,16,8,1024]{3,2,1,0:T(8,128)(2,1)} %coef_hbm.1), custom_call_target="tpu_custom_call" | custom-call | tf_op jit(solution)/shard_map/band/pallas_call | solution.py:541
  28.1 1.3 %split.1 = (f32[4,80]{1,0:T(4,128)}, f32[4,80]{1,0:T(4,128)}) custom-call(f32[8,128]{1,0:T(8,128)} %band.1.band_ref), custom_call_target="tpu_custom_call" | custom-call | tf_op jit(solution)/shard_map/split/pallas_call | solution.py:579

commit v4 on v3

--- a/solution.py
+++ b/solution.py
@@ -57,7 +57,6 @@
     frames,
     raw,
     far,
-    halo_out,
     orb,
     rest,
     pot,
@@ -176,17 +175,20 @@
             for h in range(2):
                 for f in range(per):
                     j = i + half * h
-                    if outer:
-                        p = j + depth - starts[f]
-                        p = jnp.where(p < extents[f], p, p - 2 * depth)
+                    away = j + depth - starts[f]
+                    away = jnp.where(away < extents[f], away, away - 2 * depth)
+                    near = j - starts[f]
+                    if j == depth - 1:
+                        p = odd * (near if outer else away)
+                        p += (1 - odd) * (away if outer else near)
                     else:
-                        p = j - starts[f]
+                        p = away if outer else near
                     planes.append(coef[f, jnp.clip(p, 0, box - 1)].astype(f32))
             j = i + half * upper
-            if outer:
-                masks.append((j < end_rows - depth) | (j >= start_rows + depth))
-            else:
-                masks.append((j >= start_rows) & (j < end_rows))
+            away = (j < end_rows - depth) | (j >= start_rows + depth)
+            near = (j >= start_rows) & (j < end_rows)
+            traded = (j == depth - 1) & (odd == 1)
+            masks.append(jnp.where(traded != outer, away.astype(jnp.int32), near.astype(jnp.int32)) == 1)
         stacked = jnp.concatenate(planes, 0).astype(bf16)
         fine = jnp.dot(haar_ref[...], stacked, preferred_element_type=f32)
         keep = jnp.concatenate(masks, 0)
@@ -209,7 +211,10 @@
             par, low = mate(step)
             source = frames.at[index, par * groups + low]
             target = tile_target(index, odd, me)
-            recv = main_recv.at[index // 3] if index in (0, 3) else outer_recv.at[index - 1, mine]
+            if index in (0, 3):
+                recv = main_recv.at[index // 3]
+            else:
+                recv = outer_recv.at[index - 1, mine]
             if step:
                 push(0, source, target, recv, (base + par, low))
             else:
@@ -217,6 +222,8 @@
 
     urgent = base // 2 // ((slabs + 2) // 4)
     own_first = 1 - lax.rem(urgent + odd, 2)
+
+    row_wide = iota((8, cells), 0)
 
     def relay(index, place):
         if place < 2:
@@ -242,16 +249,16 @@
 
     loads[2].wait()
     loads[3].wait()
-    build(1, True, PAIRS[0])
+    build(1, True, PAIRS[1])
     pl.semaphore_wait(barrier, team + 1)
     send_tiles(1)
     relay(1, 0)
-    build(2, True, PAIRS[1])
+    build(2, True, PAIRS[0])
     relay(2, 0)
+    send_tiles(2)
+    relay(1, 1)
     build(0, False, PAIRS[0])
     send_tiles(0)
-    send_tiles(2)
-    relay(1, 1)
     loads[4].wait()
     loads[5].wait()
     theirs = (1 - odd) * groups + me
@@ -264,7 +271,7 @@
     pick = jnp.where(at_column == plane_of(at_row) * comp + mine, 1.0, 0.0).astype(bf16)
     pot[odd] = jnp.dot(pick, own_pot, preferred_element_type=f32)
 
-    push(3, pot_out, pot_in, pot_recv, (base + 1 - odd, me))
+    push(2, pot_out, pot_in, pot_recv, (base + 1 - odd, me))
 
     build(3, False, PAIRS[1])
     send_tiles(3)
@@ -305,26 +312,9 @@
 
     for turn in range(2, 8):
         relay(1, turn)
-    arrive_main(0)
-    for side in range(2):
-        edges = [split(orb.at[side, 0, (1 + side) * groups + g])[side] for g in range(groups)]
-        for n in range(groups // 2):
-            one, two = edges[2 * n], edges[2 * n + 1]
-            for v in range(vregs):
-                if side:
-                    both = jnp.where(low_half, pltpu.roll(one[v], per, 0), two[v])
-                else:
-                    both = jnp.where(low_half, one[v], pltpu.roll(two[v], per, 0))
-                halo_out[side, 8 * n : 8 * n + 8, v * LANES : (v + 1) * LANES] = both.astype(bf16)
-        push(
-            2,
-            halo_out.at[side],
-            far.at[1 - side, 2 * groups],
-            far_recv.at[1 - side],
-            (ahead if side else behind, me),
-        )
     for turn in range(2, 8):
         relay(2, turn)
+    arrive_main(0)
     for index in (1, 2):
         arrive(tile_target(index, odd, me), outer_recv.at[index - 1, mine])
     arrive(pot_in, pot_recv)
@@ -371,13 +361,13 @@
                 both = jnp.concatenate([done[i] for i in PAIRS[t]], 0)
                 rest[side, t, at, :, v * LANES : (v + 1) * LANES] = both.astype(bf16)
 
-    def outer_frame(side, at, slot, g, up, edge, first_tile, second_tile):
+    def outer_frame(side, at, slot, g, up, edge, first, second_tile):
         begin, end = limits[slot, g, 0], limits[slot, g, 1]
         if up:
             keeps = [i + half * upper < end - depth for i in range(half)]
         else:
             keeps = [i + half * upper >= begin + depth for i in range(half)]
-        p0, p3 = split(first_tile)
+        p0, p3 = first
         p1, p2 = split(second_tile)
         planes = [select(keeps[i], p) for i, p in enumerate((p0, p1, p2, p3))]
         for v in range(vregs):
@@ -388,10 +378,10 @@
         if up:
             before, after = swap(planes[3], edge), swap(zero, planes[0])
         else:
-            before, after = swap(planes[3], zero), swap(edge, planes[0])
+            before, after = swap(planes[3], zero), swap(edge or zero, planes[0])
         finish(side, at, planes, before, after, keeps)
 
-    def main_frame(side, at, slot, g, outer_tile):
+    def main_frame(side, at, slot, g, up_tile, down_tile):
         begin, end = limits[slot, g, 0], limits[slot, g, 1]
         keeps = [
             (i + half * upper >= begin) & (i + half * upper < end) for i in range(half)
@@ -399,7 +389,7 @@
         p0, p3 = split(orb.at[side, 0, at])
         p1, p2 = split(orb.at[side, 1, at])
         planes = [p0, p1, p2, p3]
-        out0, out3 = split(outer_tile)
+        out0, out3 = split(up_tile)[0], split(down_tile)[1]
         down3 = select(half - 1 + half * upper >= begin + depth, out3)
         up0 = select(half * upper < end - depth, out0)
         finish(side, at, planes, swap(p3, down3), swap(up0, p0), keeps)
@@ -407,10 +397,15 @@
     @pl.loop(0, groups)
     def _(g):
         edge = split(orb.at[0, 0, groups + g])[1]
-        outer_frame(1, groups + g, 1, g, True, edge, raw.at[0, g], raw.at[1, g])
-        edge = split(orb.at[1, 0, 2 * groups + g])[0]
+        outer_frame(1, groups + g, 1, g, True, edge, split(raw.at[1, g]), raw.at[0, g])
         theirs = groups + g
-        outer_frame(0, groups + theirs, 2, g, False, edge, raw.at[0, theirs], raw.at[1, theirs])
+        main0, main3 = split(orb.at[1, 0, groups + theirs])
+        out0, out3 = split(raw.at[1, theirs])
+        for v in range(vregs):
+            both = jnp.concatenate([main0[v], jnp.where(low_half, main3[v], out3[v])], 0)
+            orb[1, 0, groups + theirs, :, v * LANES : (v + 1) * LANES] = both.astype(bf16)
+        out3 = [jnp.where(low_half, a, b) for a, b in zip(out3, main3)]
+        outer_frame(0, groups + theirs, 2, g, False, main0, (out0, out3), raw.at[0, theirs])
 
     quarter = lax.rem(lane8, 16) // per
     own_plane = [quarter == upper + 2 * pi for pi in range(2)]
@@ -436,13 +431,15 @@
     count = 3 * groups
     wide = count * rows_tile
 
+    def limits_wide(slot, g):
+        return jnp.concatenate([limits[slot, g, 0]] * vregs, 1)
+
     def far_side(side):
         arrive(far.at[side], far_recv.at[side])
         for g in range(groups):
-            edge = split(far.at[side, 2 * groups])[g // 2]
-            if g % 2 == side:
-                edge = [pltpu.roll(x, per, 0) for x in edge]
-            outer_frame(side, g, 3 * side, g, not side, edge, far.at[side, g], far.at[side, groups + g])
+            edge = None if side else split(far.at[0, groups + g])[1]
+            first, second = split(far.at[side, groups + g]), far.at[side, g]
+            outer_frame(side, g, 3 * side, g, not side, edge, first, second)
 
     def products(side):
         for t in range(2):
@@ -459,6 +456,21 @@
                 acc[side] += part
             else:
                 acc[side] = part
+        if side == 0:
+            tops = []
+            for g in range(groups):
+                plane0 = pltpu.roll(orb[0, 0, groups + g][:8].astype(f32), per, 0)
+                here = (row_wide >= per) & (limits_wide(1, g) < 0)
+                plane0 = jnp.where(here, -0.5 * plane0, 0.0)
+                tops += [jnp.zeros((8, cells), f32), plane0]
+            others = [far[0, groups + g] for g in range(groups)] + [raw[1, g] for g in range(groups)]
+            top = (count + groups) * rows_tile
+            acc[0, top : top + groups * rows_tile, :LANES] += lax.dot_general(
+                jnp.concatenate(tops, 0).astype(bf16),
+                jnp.concatenate(others, 0),
+                (((1,), (1,)), ((), ())),
+                preferred_element_type=f32,
+            )
         for g in range(groups):
             one, two = gathered(side, g)
             if side:
@@ -471,8 +483,9 @@
     arrive_main(1)
     @pl.loop(0, groups)
     def _(g):
-        main_frame(0, groups + g, 1, g, raw.at[0, g])
-        main_frame(1, 2 * groups + g, 2, g, raw.at[0, groups + g])
+        main_frame(0, groups + g, 1, g, raw.at[1, g], raw.at[1, g])
+        own = 2 * groups + g
+        main_frame(1, own, 2, g, raw.at[1, groups + g], orb.at[0, 0, own])
     for turn in range(2):
         now = urgent + turn - 2 * urgent * turn
         for side in range(2):
@@ -481,7 +494,7 @@
             pl.when(now == side)(functools.partial(products, side))
         for g in range(groups):
             push(
-                4,
+                3,
                 rows.at[3 * now, g],
                 got_rows.at[team + mine],
                 rows_recv,
@@ -498,7 +511,7 @@
         par, low = mate(step)
         source, target = rows.at[1 + par, low], got_rows.at[mine]
         if step:
-            push(4, source, target, rows_recv, (base + par, low))
+            push(3, source, target, rows_recv, (base + par, low))
         else:
             pltpu.make_async_copy(source, target, rows_recv).start()
     arrive(got_rows, rows_recv)
@@ -516,7 +529,7 @@
     ) * (1.0 / comp)
     out_ref[...] = total + jnp.where(low_half, 0.0, 3.0 * pltpu.roll(total, per, 0))
     for kind, block in enumerate(
-        (frames.at[:, : comp - 1], raw, halo_out, pot_out, got_rows.at[: 2 * team - 1])
+        (frames.at[:, : comp - 1], raw, pot_out, got_rows.at[: 2 * team - 1])
     ):
         arrive(block, sent_sem.at[kind])
 
@@ -552,8 +565,7 @@
             pltpu.VMEM((per, box, comp, cells), bf16),
             tiles(4, comp),
             tiles(2, team),
-            tiles(2, 2 * groups + 1),
-            tiles(2),
+            tiles(2, 2 * groups),
             tiles(2, 2, 3 * groups),
             tiles(2, 2, 3 * groups),
             pltpu.VMEM((2, 4 * depth, cells), f32),
@@ -565,7 +577,7 @@
             pltpu.VMEM((4, groups, 2 * per, LANES), f32),
             pltpu.VMEM((2 * team, 2 * per, LANES), f32),
             dma((6,)),
-            dma((5,)),
+            dma((4,)),
             dma,
             dma((2, team)),
             dma((2,)),

time: 29.6 us -> 28.3 us (0.956)
  Pallas kernels: 28.8 us -> 27.5 us
    pallas_call x1, Pallas kernels: 27.5 us -> 26.2 us  [local(): pl.pallas_call(functools.partial(band_kernel, slabs, groups, depth), out_...]
where the time goes in v4:
time: 28.3 us; the launch traced here: 28.1 us
  Pallas kernels  27.5 us (97%)
  between operations  0.64 us (2%)
    pallas_call x1, Pallas kernels, local(): pl.pallas_call(functools.partial(band_kernel, slabs, groups, depth), out_...  26.2 us
    pallas_call x1, Pallas kernels, local(): pl.pallas_call(split_kernel, out_shape=(out, out), in_specs=[vmem], out_s...  1.27 us

profile of v4, /device:TPU:0, one launch (start us, length us, event | category | flops | bytes accessed | tf_op | source)
XLA Modules:
  0.0 28.1 jit_solution(17823419347397864247)
XLA Ops:
  0.6 26.2 %band.1.band_ref = f32[8,128]{1,0:T(8,128)} custom-call(bf16[8,8,1024]{2,1,0:T(8,128)(2,1)} %pot_hbm.1, s32[128]{0:T(128)} %center_hbm.1, s32[128]{0:T(128)} %extent_hbm.1, bf16[128,128]{1,0:T(8,128)(2,1)} %constant.4.clone.haar_hbm, bf16[256,256]{1,0:T(8,128)(2,1)} %constant.5.clone.lap_hbm, bf16[4,16,8,1024]{3,2,1,0:T(8,128)(2,1)} %coef_hbm.1), custom_call_target="tpu_custom_call" | custom-call | tf_op jit(solution)/shard_map/band/pallas_call | solution.py:554
  26.8 1.3 %split.1 = (f32[4,80]{1,0:T(4,128)}, f32[4,80]{1,0:T(4,128)}) custom-call(f32[8,128]{1,0:T(8,128)} %band.1.band_ref), custom_call_target="tpu_custom_call" | custom-call | tf_op jit(solution)/shard_map/split/pallas_call | solution.py:591

commit v5 on v4

--- a/solution.py
+++ b/solution.py
@@ -206,15 +206,18 @@
     def arrive_main(index):
         arrive(frames.at[0], main_recv.at[index])
 
-    def send_tiles(index):
+    def piece(ref, part):
+        return ref if part is None else ref.at[:, part * cells // 2 : (part + 1) * cells // 2]
+
+    def send_tiles(index, part=None):
         for step in steps:
             par, low = mate(step)
-            source = frames.at[index, par * groups + low]
-            target = tile_target(index, odd, me)
+            source = piece(frames.at[index, par * groups + low], part)
+            target = piece(tile_target(index, odd, me), part)
             if index in (0, 3):
                 recv = main_recv.at[index // 3]
             else:
-                recv = outer_recv.at[index - 1, mine]
+                recv = outer_recv.at[2 * index - 2 if part is None else part, mine]
             if step:
                 push(0, source, target, recv, (base + par, low))
             else:
@@ -225,7 +228,7 @@
 
     row_wide = iota((8, cells), 0)
 
-    def relay(index, place):
+    def relay(index, place, part=None):
         if place < 2:
             par, low = mate(place)
         else:
@@ -235,14 +238,15 @@
             second = mate((0, 1, 2, 3, 2, 3)[place - 2])[1]
             low = own_first * first + (1 - own_first) * second
         if place:
-            block = tile_target(index, par, low)
-            arrive(block, outer_recv.at[index - 1, par * groups + low])
+            block = piece(tile_target(index, par, low), part)
+            row = 2 * index - 2 if part is None else part
+            arrive(block, outer_recv.at[row, par * groups + low])
         else:
-            block = frames.at[index, mine]
+            block = piece(frames.at[index, mine], part)
         push(
             1,
             block,
-            far.at[1 - par, (index - 1) * groups + low],
+            piece(far.at[1 - par, (index - 1) * groups + low], part),
             far_recv.at[1 - par],
             (lax.rem(slab + slabs + 4 * par - 2, slabs), me),
         )
@@ -251,14 +255,14 @@
     loads[3].wait()
     build(1, True, PAIRS[1])
     pl.semaphore_wait(barrier, team + 1)
-    send_tiles(1)
+    send_tiles(1, 0)
+    send_tiles(1, 1)
     relay(1, 0)
     build(2, True, PAIRS[0])
     relay(2, 0)
     send_tiles(2)
-    relay(1, 1)
-    build(0, False, PAIRS[0])
-    send_tiles(0)
+    relay(1, 1, 0)
+    relay(1, 1, 1)
     loads[4].wait()
     loads[5].wait()
     theirs = (1 - odd) * groups + me
@@ -272,6 +276,8 @@
     pot[odd] = jnp.dot(pick, own_pot, preferred_element_type=f32)
 
     push(2, pot_out, pot_in, pot_recv, (base + 1 - odd, me))
+    build(0, False, PAIRS[0])
+    send_tiles(0)
 
     build(3, False, PAIRS[1])
     send_tiles(3)
@@ -292,11 +298,10 @@
     at_row, at_column = iota((2 * LANES, LANES), 0), iota((2 * LANES, LANES), 1)
     lane = lax.rem(at_row, LANES)
     slot_of = lane // 64 + 2 * (lax.rem(lane, 8 * 2) // 8)
-    member = lax.rem(lane, 64) // 16 * per + lax.rem(lane, 8)
+    member = lax.rem(lane, 64) // 16 * per + lax.rem(lane, per)
     near = at_row < LANES
     band = jnp.where(near, slot_of + 1 - odd, slot_of - 1 + 3 * odd)
-    fits = (lax.rem(lane, 8) < per) & (band >= 0) & (band < 5)
-    fits = fits & (at_column == band * groups * per + member)
+    fits = (band >= 0) & (band < 5) & (at_column == band * groups * per + member)
     place[...] = jnp.where(fits, 1.0, 0.0)
 
     low_half = row8 < per
@@ -310,13 +315,15 @@
         cut = lambda part: [part[:, v * LANES : (v + 1) * LANES] for v in range(vregs)]
         return cut(wide[:8]), cut(wide[8:])
 
-    for turn in range(2, 8):
-        relay(1, turn)
+    for part in range(2):
+        for turn in range(2, 8):
+            relay(1, turn, part)
     for turn in range(2, 8):
         relay(2, turn)
     arrive_main(0)
-    for index in (1, 2):
-        arrive(tile_target(index, odd, me), outer_recv.at[index - 1, mine])
+    for part in range(2):
+        arrive(piece(tile_target(1, odd, me), part), outer_recv.at[part, mine])
+    arrive(tile_target(2, odd, me), outer_recv.at[2, mine])
     arrive(pot_in, pot_recv)
     padded = jnp.concatenate([pot_in[...].astype(f32), jnp.zeros((depth, cells), f32)], 0)
     at_row, at_column = iota((4 * depth, 2 * depth), 0), iota((4 * depth, 2 * depth), 1)
@@ -361,12 +368,12 @@
                 both = jnp.concatenate([done[i] for i in PAIRS[t]], 0)
                 rest[side, t, at, :, v * LANES : (v + 1) * LANES] = both.astype(bf16)
 
-    def outer_frame(side, at, slot, g, up, edge, first, second_tile):
+    def outer_frame(side, at, slot, g, up, below, above, first, second_tile):
         begin, end = limits[slot, g, 0], limits[slot, g, 1]
-        if up:
-            keeps = [i + half * upper < end - depth for i in range(half)]
-        else:
-            keeps = [i + half * upper >= begin + depth for i in range(half)]
+        low, high = (-box, end - depth) if up else (begin + depth, box)
+        keeps = [
+            (i + half * upper >= low) & (i + half * upper < high) for i in range(half)
+        ]
         p0, p3 = first
         p1, p2 = split(second_tile)
         planes = [select(keeps[i], p) for i, p in enumerate((p0, p1, p2, p3))]
@@ -375,10 +382,7 @@
                 both = jnp.concatenate([planes[i][v] for i in PAIRS[t]], 0)
                 orb[side, t, at, :, v * LANES : (v + 1) * LANES] = both.astype(bf16)
         zero = [jnp.zeros((8, LANES), f32)] * vregs
-        if up:
-            before, after = swap(planes[3], edge), swap(zero, planes[0])
-        else:
-            before, after = swap(planes[3], zero), swap(edge or zero, planes[0])
+        before, after = swap(planes[3], below or zero), swap(above or zero, planes[0])
         finish(side, at, planes, before, after, keeps)
 
     def main_frame(side, at, slot, g, up_tile, down_tile):
@@ -397,7 +401,7 @@
     @pl.loop(0, groups)
     def _(g):
         edge = split(orb.at[0, 0, groups + g])[1]
-        outer_frame(1, groups + g, 1, g, True, edge, split(raw.at[1, g]), raw.at[0, g])
+        outer_frame(1, groups + g, 1, g, True, edge, None, split(raw.at[1, g]), raw.at[0, g])
         theirs = groups + g
         main0, main3 = split(orb.at[1, 0, groups + theirs])
         out0, out3 = split(raw.at[1, theirs])
@@ -405,26 +409,27 @@
             both = jnp.concatenate([main0[v], jnp.where(low_half, main3[v], out3[v])], 0)
             orb[1, 0, groups + theirs, :, v * LANES : (v + 1) * LANES] = both.astype(bf16)
         out3 = [jnp.where(low_half, a, b) for a, b in zip(out3, main3)]
-        outer_frame(0, groups + theirs, 2, g, False, main0, (out0, out3), raw.at[0, theirs])
+        outer_frame(
+            0, groups + theirs, 2, g, False, None, main0, (out0, out3), raw.at[0, theirs]
+        )
 
     quarter = lax.rem(lane8, 16) // per
     own_plane = [quarter == upper + 2 * pi for pi in range(2)]
 
-    def gathered(side, at):
+    def own_planes(side, at, v):
         both = []
         for kind in range(2):
             top = (kind * count + at) * rows_tile
-            parts = []
-            for v in range(2):
-                lanes = slice(v * LANES, (v + 1) * LANES)
-                value = jnp.where(own_plane[0], acc[side, top : top + 8, lanes], 0.0)
-                value += jnp.where(own_plane[1], acc[side, top + 8 : top + 16, lanes], 0.0)
-                value += pltpu.roll(value, per, 0)
-                value += pltpu.roll(value, LANES - 4, 1)
-                value += pltpu.roll(value, LANES - 8, 1)
-                parts.append(value)
-            both.append(parts)
-        return [jnp.where(low_half, both[0][v], both[1][v]) for v in range(2)]
+            lanes = slice(v * LANES, (v + 1) * LANES)
+            value = jnp.where(own_plane[0], acc[side, top : top + 8, lanes], 0.0)
+            both.append(value + jnp.where(own_plane[1], acc[side, top + 8 : top + 16, lanes], 0.0))
+        return both
+
+    def folded(both):
+        margin, image = both
+        value = jnp.where(low_half, margin, image)
+        value += pltpu.roll(jnp.where(low_half, image, margin), per, 0)
+        return value + pltpu.roll(value, LANES - 8, 1)
 
     left = lane8 < LANES // 2
     even = lax.rem(lane8, 16) < 8
@@ -434,78 +439,93 @@
     def limits_wide(slot, g):
         return jnp.concatenate([limits[slot, g, 0]] * vregs, 1)
 
-    def far_side(side):
+    def far_frames(side):
         arrive(far.at[side], far_recv.at[side])
         for g in range(groups):
-            edge = None if side else split(far.at[0, groups + g])[1]
-            first, second = split(far.at[side, groups + g]), far.at[side, g]
-            outer_frame(side, g, 3 * side, g, not side, edge, first, second)
-
-    def products(side):
+            first = split(far.at[side, groups + g])
+            below = None if side else first[1]
+            outer_frame(side, g, 3 * side, g, not side, below, None, first, far.at[side, g])
+
+    def main_frames(side):
+        for g in range(groups):
+            at = (1 + side) * groups + g
+            down = orb.at[0, 0, at] if side else raw.at[1, g]
+            main_frame(side, at, 1 + side, g, raw.at[1, side * groups + g], down)
+
+    def meet(side):
         for t in range(2):
             columns = orb[side, t].reshape(wide, cells)
-            images = rest[side, t].reshape(wide, cells)
-            full = jnp.concatenate([columns, columns[: 2 * LANES - wide]], 0)
             part = lax.dot_general(
-                jnp.concatenate([columns, images], 0),
-                full,
+                jnp.concatenate([columns, rest[side, t].reshape(wide, cells)], 0),
+                columns,
                 (((1,), (1,)), ((), ())),
                 preferred_element_type=f32,
             )
             if t:
-                acc[side] += part
+                acc[side, :, :wide] += part
             else:
-                acc[side] = part
-        if side == 0:
-            tops = []
-            for g in range(groups):
-                plane0 = pltpu.roll(orb[0, 0, groups + g][:8].astype(f32), per, 0)
-                here = (row_wide >= per) & (limits_wide(1, g) < 0)
-                plane0 = jnp.where(here, -0.5 * plane0, 0.0)
-                tops += [jnp.zeros((8, cells), f32), plane0]
-            others = [far[0, groups + g] for g in range(groups)] + [raw[1, g] for g in range(groups)]
-            top = (count + groups) * rows_tile
-            acc[0, top : top + groups * rows_tile, :LANES] += lax.dot_general(
-                jnp.concatenate(tops, 0).astype(bf16),
-                jnp.concatenate(others, 0),
-                (((1,), (1,)), ((), ())),
-                preferred_element_type=f32,
-            )
+                acc[side, :, :wide] = part
         for g in range(groups):
-            one, two = gathered(side, g)
-            if side:
-                near_cols = jnp.where(left, 0.0, one)
-                far_cols = jnp.where(left, two, pltpu.roll(one, LANES // 2, 1))
-            else:
-                near_cols, far_cols = one, jnp.where(left, two, 0.0)
+            one, two = folded(own_planes(side, g, 0)), folded(own_planes(side, g, 1))
+            turned = pltpu.roll(one, LANES // 2, 1) if side else 0.0
+            near_cols = jnp.where(left, 0.0, one) if side else one
+            far_cols = jnp.where(left, two, turned)
             rows[3 * side, g] = jnp.where(even, near_cols, pltpu.roll(far_cols, 8, 1))
 
-    arrive_main(1)
-    @pl.loop(0, groups)
-    def _(g):
-        main_frame(0, groups + g, 1, g, raw.at[1, g], raw.at[1, g])
-        own = 2 * groups + g
-        main_frame(1, own, 2, g, raw.at[1, groups + g], orb.at[0, 0, own])
-    for turn in range(2):
-        now = urgent + turn - 2 * urgent * turn
-        for side in range(2):
-            pl.when(now == side)(functools.partial(far_side, side))
-        for side in range(2):
-            pl.when(now == side)(functools.partial(products, side))
         for g in range(groups):
             push(
                 3,
-                rows.at[3 * now, g],
+                rows.at[3 * side, g],
                 got_rows.at[team + mine],
                 rows_recv,
-                (lax.rem(base + slabs - 1 + 3 * now, slabs), g),
+                (lax.rem(base + slabs - 1 + 3 * side, slabs), g),
             )
+
+    def at_end(first):
+        arrive_main(1)
+        main_frames(first)
+        far_frames(first)
+        meet(first)
+        main_frames(1 - first)
+        far_frames(1 - first)
+        meet(1 - first)
+
+    def between():
+        arrive_main(1)
+        for side in range(2):
+            main_frames(side)
+        for side in range(2):
+            far_frames(side)
+            meet(side)
+
+    pl.when(base == 0)(functools.partial(at_end, 0))
+    pl.when(base == slabs - 2)(functools.partial(at_end, 1))
+    pl.when((base > 0) & (base < slabs - 2))(between)
+
+    tops = []
+    for g in range(groups):
+        plane0 = pltpu.roll(orb[0, 0, groups + g][:8].astype(f32), per, 0)
+        here = (row_wide >= per) & (limits_wide(1, g) < 0)
+        tops += [jnp.zeros((8, cells), f32), jnp.where(here, -0.5 * plane0, 0.0)]
+    others = [far[0, groups + g] for g in range(groups)] + [raw[1, g] for g in range(groups)]
+    top = (count + groups) * rows_tile
+    acc[0, top : top + groups * rows_tile, :LANES] += lax.dot_general(
+        jnp.concatenate(tops, 0).astype(bf16),
+        jnp.concatenate(others, 0),
+        (((1,), (1,)), ((), ())),
+        preferred_element_type=f32,
+    )
     for slot in (1, 2):
         for g in range(groups):
-            v0, v1 = gathered(0, slot * groups + g)
-            w0, w1 = gathered(1, slot * groups + g)
-            near_cols = jnp.where(left, v0, v0 + w0)
-            far_cols = jnp.where(left, v1 + w1, pltpu.roll(w0, LANES // 2, 1))
+            at = slot * groups + g
+            pair = [own_planes(side, at, 0) for side in range(2)]
+            last = [own_planes(side, at, 1) for side in range(2)]
+            near_cols = [jnp.where(left, v, v + w) for v, w in zip(*pair)]
+            far_cols = [
+                jnp.where(left, v + w, pltpu.roll(x, LANES // 2, 1))
+                for v, w, x in zip(*last, pair[1])
+            ]
+            near_cols, far_cols = folded(near_cols), folded(far_cols)
             rows[slot, g] = jnp.where(even, near_cols, pltpu.roll(far_cols, 8, 1))
     for step in steps:
         par, low = mate(step)
@@ -579,7 +599,7 @@
             dma((6,)),
             dma((4,)),
             dma,
-            dma((2, team)),
+            dma((3, team)),
             dma((2,)),
             dma((2,)),
             dma,

time: 28.3 us -> 27.7 us (0.979)
  Pallas kernels: 27.5 us -> 26.8 us
    pallas_call x1, Pallas kernels: 26.2 us -> 25.6 us  [local(): pl.pallas_call(functools.partial(band_kernel, slabs, groups, depth), out_...]
where the time goes in v5:
time: 27.7 us; the launch traced here: 27.5 us
  Pallas kernels  26.8 us (97%)
  between operations  0.64 us (2%)
    pallas_call x1, Pallas kernels, local(): pl.pallas_call(functools.partial(band_kernel, slabs, groups, depth), out_...  25.6 us
    pallas_call x1, Pallas kernels, local(): pl.pallas_call(split_kernel, out_shape=(out, out), in_specs=[vmem], out_s...  1.27 us

profile of v5, /device:TPU:0, one launch (start us, length us, event | category | flops | bytes accessed | tf_op | source)
XLA Modules:
  0.0 27.5 jit_solution(6448601360364038084)
XLA Ops:
  0.6 25.6 %band.1.band_ref = f32[8,128]{1,0:T(8,128)} custom-call(bf16[8,8,1024]{2,1,0:T(8,128)(2,1)} %pot_hbm.1, s32[128]{0:T(128)} %center_hbm.1, s32[128]{0:T(128)} %extent_hbm.1, bf16[128,128]{1,0:T(8,128)(2,1)} %constant.4.clone.haar_hbm, bf16[256,256]{1,0:T(8,128)(2,1)} %constant.5.clone.lap_hbm, bf16[4,16,8,1024]{3,2,1,0:T(8,128)(2,1)} %coef_hbm.1), custom_call_target="tpu_custom_call" | custom-call | tf_op jit(solution)/shard_map/band/pallas_call | solution.py:574
  26.2 1.3 %split.1 = (f32[4,80]{1,0:T(4,128)}, f32[4,80]{1,0:T(4,128)}) custom-call(f32[8,128]{1,0:T(8,128)} %band.1.band_ref), custom_call_target="tpu_custom_call" | custom-call | tf_op jit(solution)/shard_map/split/pallas_call | solution.py:611

commit v6 on v5

--- a/solution.py
+++ b/solution.py
@@ -67,6 +67,7 @@
     place,
     rows,
     got_rows,
+    owed,
     load_sem,
     sent_sem,
     pot_recv,
@@ -320,6 +321,34 @@
             relay(1, turn, part)
     for turn in range(2, 8):
         relay(2, turn)
+    def lane_tiles(wide):
+        return [wide[:, v * LANES : (v + 1) * LANES] for v in range(vregs)]
+
+    def squares(n, exact):
+        for f in range(per):
+            value = coef[f, n].astype(f32)
+            value = functools.reduce(jnp.add, lane_tiles(value * value))
+            inside = jnp.full((8, LANES), n, jnp.int32) < extents[f]
+            exact = exact[:f] + [exact[f] + jnp.where(inside, value, 0.0)] + exact[f + 1 :]
+        return exact
+
+    def fine_squares(n, rounded):
+        for index in range(4):
+            for top in (0, 8):
+                value = frames[index, n, top : top + 8].astype(f32)
+                rounded = rounded + functools.reduce(jnp.add, lane_tiles(value * value))
+        return rounded
+
+    zeros = jnp.zeros((8, LANES), f32)
+    exact = lax.fori_loop(0, box, squares, [zeros] * per)
+    rounded = lax.fori_loop(0, comp, fine_squares, zeros)
+    lost = jnp.sum(rounded, axis=1, keepdims=True) * (-1.0 / comp)
+    lost = lost + pltpu.roll(jnp.broadcast_to(lost, (8, LANES)), per, 0)
+    for f in range(per):
+        lost = lost + jnp.where(row8 == f, jnp.sum(exact[f]), 0.0)
+    at_home = lane8 == 2 * groups * per + me * per + row8
+    owed[...] = jnp.where((row8 < per) & at_home, lost, 0.0)
+
     arrive_main(0)
     for part in range(2):
         arrive(piece(tile_target(1, odd, me), part), outer_recv.at[part, mine])
@@ -546,7 +575,7 @@
         place[...],
         preferred_element_type=f32,
         precision=lax.Precision.HIGHEST,
-    ) * (1.0 / comp)
+    ) * (1.0 / comp) + owed[...]
     out_ref[...] = total + jnp.where(low_half, 0.0, 3.0 * pltpu.roll(total, per, 0))
     for kind, block in enumerate(
         (frames.at[:, : comp - 1], raw, pot_out, got_rows.at[: 2 * team - 1])
@@ -596,6 +625,7 @@
             pltpu.VMEM((2 * LANES, LANES), f32),
             pltpu.VMEM((4, groups, 2 * per, LANES), f32),
             pltpu.VMEM((2 * team, 2 * per, LANES), f32),
+            pltpu.VMEM((2 * per, LANES), f32),
             dma((6,)),
             dma((4,)),
             dma,

time: 27.7 us -> 27.7 us (level)
  no operation moved by 1% of the time
where the time goes in v6:
time: 27.7 us; the launch traced here: 27.5 us
  Pallas kernels  26.9 us (97%)
  between operations  0.64 us (2%)
    pallas_call x1, Pallas kernels, local(): pl.pallas_call(functools.partial(band_kernel, slabs, groups, depth), out_...  25.6 us
    pallas_call x1, Pallas kernels, local(): pl.pallas_call(split_kernel, out_shape=(out, out), in_specs=[vmem], out_s...  1.27 us

profile of v6, /device:TPU:0, one launch (start us, length us, event | category | flops | bytes accessed | tf_op | source)
XLA Modules:
  0.0 27.5 jit_solution(11885068831257923549)
XLA Ops:
  0.6 25.6 %band.1.band_ref = f32[8,128]{1,0:T(8,128)} custom-call(bf16[8,8,1024]{2,1,0:T(8,128)(2,1)} %pot_hbm.1, s32[128]{0:T(128)} %center_hbm.1, s32[128]{0:T(128)} %extent_hbm.1, bf16[128,128]{1,0:T(8,128)(2,1)} %constant.4.clone.haar_hbm, bf16[256,256]{1,0:T(8,128)(2,1)} %constant.5.clone.lap_hbm, bf16[4,16,8,1024]{3,2,1,0:T(8,128)(2,1)} %coef_hbm.1), custom_call_target="tpu_custom_call" | custom-call | tf_op jit(solution)/shard_map/band/pallas_call | solution.py:603
  26.2 1.3 %split.1 = (f32[4,80]{1,0:T(4,128)}, f32[4,80]{1,0:T(4,128)}) custom-call(f32[8,128]{1,0:T(8,128)} %band.1.band_ref), custom_call_target="tpu_custom_call" | custom-call | tf_op jit(solution)/shard_map/split/pallas_call | solution.py:641
